TPU v7x, 32 devices: a whole 2x2x4 slice. The times are simulated.
32 devices in a mesh: dp: 4 (over z), fsdp: 8 (over y, x, core).
Axes of the slice: x: 2, y: 2, z: 4, core: 2. Of those that a mesh axis runs over, the one named last changes fastest.
Arguments:
- dec_in: bfloat16 [64, 176, 768], P(('dp', 'fsdp')), may hold values from -6 to 6
- enc_out: bfloat16 [64, 512, 768], P(('dp', 'fsdp')), may hold values from -6 to 6
- seg_dec: int32 [64, 176], P(('dp', 'fsdp')), may hold values from 0 to 4, as said below
- seg_enc: int32 [64, 512], P(('dp', 'fsdp')), may hold values from 0 to 4, as said below
- out_grad: bfloat16 [64, 176, 768], P(('dp', 'fsdp')), may hold values from -6 to 6
- gain_self: bfloat16 [768], P('fsdp'), may hold values from 0.099609375 to 1.8984375
- wq_self: bfloat16 [768, 768], P('fsdp'), may hold values from -0.21875 to 0.21875
- wk_self: bfloat16 [768, 768], P('fsdp'), may hold values from -0.21875 to 0.21875
- wv_self: bfloat16 [768, 768], P('fsdp'), may hold values from -0.21875 to 0.21875
- wo_self: bfloat16 [768, 768], P('fsdp'), may hold values from -1.5 to 1.5
- gain_cross: bfloat16 [768], P('fsdp'), may hold values from 0.099609375 to 1.8984375
- wq_cross: bfloat16 [768, 768], P('fsdp'), may hold values from -0.21875 to 0.21875
- wk_cross: bfloat16 [768, 768], P('fsdp'), may hold values from -0.21875 to 0.21875
- wv_cross: bfloat16 [768, 768], P('fsdp'), may hold values from -0.21875 to 0.21875
- wo_cross: bfloat16 [768, 768], P('fsdp'), may hold values from -2.5 to 2.5
- gain_ffn: bfloat16 [768], P('fsdp'), may hold values from 0.099609375 to 1.8984375
- w_gate: bfloat16 [768, 2048], P('fsdp'), may hold values from -0.21875 to 0.21875
- w_up: bfloat16 [768, 2048], P('fsdp'), may hold values from -0.21875 to 0.21875
- w_down: bfloat16 [2048, 768], P('fsdp'), may hold values from -0.125 to 0.125
Outputs:
- dec_out: bfloat16 [64, 176, 768], P(('dp', 'fsdp'))
- grad_dec: float32 [64, 176, 768], P(('dp', 'fsdp'))
- grad_enc: float32 [64, 512, 768], P(('dp', 'fsdp'))
- grad_gain_self: float32 [768], P('fsdp')
- grad_wq_self: float32 [768, 768], P('fsdp')
- grad_wk_self: float32 [768, 768], P('fsdp')
- grad_wv_self: float32 [768, 768], P('fsdp')
- grad_wo_self: float32 [768, 768], P('fsdp')
- grad_gain_cross: float32 [768], P('fsdp')
- grad_wq_cross: float32 [768, 768], P('fsdp')
- grad_wk_cross: float32 [768, 768], P('fsdp')
- grad_wv_cross: float32 [768, 768], P('fsdp')
- grad_wo_cross: float32 [768, 768], P('fsdp')
- grad_gain_ffn: float32 [768], P('fsdp')
- grad_w_gate: float32 [768, 2048], P('fsdp')
- grad_w_up: float32 [768, 2048], P('fsdp')
- grad_w_down: float32 [2048, 768], P('fsdp')
Inputs may be any that keep to these rules, and one draw needn't show every extreme that they name: `seg_dec`: each row holds segments 1, 2, 3, 4 in this order, each present in both its decoder and its encoder tokens, then 1 to 176 // 16 (decoder) or 512 // 16 (encoder) padding tokens of segment 0 at its end. `seg_enc`: as for seg_dec, with the same segments present.
All inputs are finite; a program needn't handle non-finite values.
Results may differ from a plain program's by a relative error of at most 0.023.
Values may be sent and summed in bfloat16 or wider, within the bound.
A program may use at most 192 MiB of HBM per device.

v0:
```python
import jax
import jax.numpy as jnp
from jax import lax
from jax.sharding import PartitionSpec as P

HD = 64
MICRO = 2


EPSILON = 1e-06
MASKED = -1000000000.0


def rms_forward(values_in, gain_vec):
    return (
        values_in
        * lax.rsqrt(jnp.mean(values_in * values_in, axis=-1, keepdims=True) + EPSILON)
        * gain_vec
    )


def rms_backward(values_in, gain_low, grad_out):
    _, pullback = jax.vjp(rms_forward, values_in, gain_low.astype(jnp.float32))
    return pullback(grad_out)


def project(acts, weight):
    return jnp.einsum("rld,dn->rln", acts, weight, preferred_element_type=jnp.float32)


def weight_grad(acts, grad_out):
    return jnp.einsum("rld,rln->dn", acts, grad_out, preferred_element_type=jnp.float32)


def input_grad(grad_out, weight):
    return jnp.einsum("rln,dn->rld", grad_out, weight, preferred_element_type=jnp.float32)


def split_heads(tensor):
    return tensor.reshape(tensor.shape[0], tensor.shape[1], -1, HD)


def merge_heads(tensor):
    return tensor.reshape(tensor.shape[0], tensor.shape[1], -1)


def masked_scores(queries, keys_all, allowed):
    raw_scores = jnp.einsum(
        "rqhd,rkhd->rhqk",
        split_heads(queries),
        split_heads(keys_all),
        preferred_element_type=jnp.float32,
    ) * HD ** (-0.5)
    return jnp.where(allowed[:, None], raw_scores, MASKED)


def attend_forward(queries, keys_all, values, allowed):
    scores = masked_scores(queries, keys_all, allowed)
    maxima = jnp.max(scores, axis=-1, keepdims=True)
    log_total = maxima + jnp.log(jnp.sum(jnp.exp(scores - maxima), axis=-1, keepdims=True))
    weights_low = jnp.exp(scores - log_total).astype(jnp.bfloat16)
    mixture = jnp.einsum(
        "rhqk,rkhd->rqhd", weights_low, split_heads(values), preferred_element_type=jnp.float32
    )
    return (merge_heads(mixture).astype(jnp.bfloat16), log_total)


def attend_backward(queries, keys_all, values, allowed, log_total, grad_mix):
    scores = masked_scores(queries, keys_all, allowed)
    weights_full = jnp.exp(scores - log_total)
    grad_heads = split_heads(grad_mix)
    grad_values = jnp.einsum(
        "rhqk,rqhd->rkhd",
        weights_full.astype(jnp.bfloat16),
        grad_heads,
        preferred_element_type=jnp.float32,
    )
    grad_weights = jnp.einsum(
        "rqhd,rkhd->rhqk", grad_heads, split_heads(values), preferred_element_type=jnp.float32
    )
    grad_scores = (
        weights_full * (grad_weights - jnp.sum(weights_full * grad_weights, axis=-1, keepdims=True))
    ).astype(jnp.bfloat16)
    grad_queries = jnp.einsum(
        "rhqk,rkhd->rqhd", grad_scores, split_heads(keys_all), preferred_element_type=jnp.float32
    ) * HD ** (-0.5)
    grad_keys = jnp.einsum(
        "rhqk,rqhd->rkhd", grad_scores, split_heads(queries), preferred_element_type=jnp.float32
    ) * HD ** (-0.5)
    return (
        merge_heads(grad_queries).astype(jnp.bfloat16),
        merge_heads(grad_keys).astype(jnp.bfloat16),
        merge_heads(grad_values).astype(jnp.bfloat16),
    )


def fetch_self(gain_vec, query_w, key_w, value_w, output_w):
    return (
        lax.all_gather(gain_vec, "fsdp", axis=0, tiled=True),
        lax.all_gather(query_w, "fsdp", axis=0, tiled=True),
        lax.all_gather(key_w, "fsdp", axis=0, tiled=True),
        lax.all_gather(value_w, "fsdp", axis=0, tiled=True),
        lax.all_gather(output_w, "fsdp", axis=0, tiled=True),
    )


def fetch_cross(gain_vec, query_w, key_w, value_w, output_w):
    return (
        lax.all_gather(gain_vec, "fsdp", axis=0, tiled=True),
        lax.all_gather(query_w, "fsdp", axis=0, tiled=True),
        lax.all_gather(key_w, "fsdp", axis=0, tiled=True),
        lax.all_gather(value_w, "fsdp", axis=0, tiled=True),
        lax.all_gather(output_w, "fsdp", axis=0, tiled=True),
    )


def fetch_ffn(gain_vec, gate_w, up_w, down_w):
    return (
        lax.all_gather(gain_vec, "fsdp", axis=0, tiled=True),
        lax.all_gather(gate_w, "fsdp", axis=0, tiled=True),
        lax.all_gather(up_w, "fsdp", axis=0, tiled=True),
        lax.all_gather(down_w, "fsdp", axis=0, tiled=True),
    )


def share_self(gradients):
    return tuple(
        (
            lax.psum_scatter(gradients[0], "fsdp", scatter_dimension=0, tiled=True),
            lax.psum_scatter(gradients[1], "fsdp", scatter_dimension=0, tiled=True),
            lax.psum_scatter(gradients[2], "fsdp", scatter_dimension=0, tiled=True),
            lax.psum_scatter(gradients[3], "fsdp", scatter_dimension=0, tiled=True),
            lax.psum_scatter(gradients[4], "fsdp", scatter_dimension=0, tiled=True),
        )
    )


def share_cross(gradients):
    return tuple(
        (
            lax.psum_scatter(gradients[0], "fsdp", scatter_dimension=0, tiled=True),
            lax.psum_scatter(gradients[1], "fsdp", scatter_dimension=0, tiled=True),
            lax.psum_scatter(gradients[2], "fsdp", scatter_dimension=0, tiled=True),
            lax.psum_scatter(gradients[3], "fsdp", scatter_dimension=0, tiled=True),
            lax.psum_scatter(gradients[4], "fsdp", scatter_dimension=0, tiled=True),
        )
    )


def share_ffn(gradients):
    return tuple(
        (
            lax.psum_scatter(gradients[0], "fsdp", scatter_dimension=0, tiled=True),
            lax.psum_scatter(gradients[1], "fsdp", scatter_dimension=0, tiled=True),
            lax.psum_scatter(gradients[2], "fsdp", scatter_dimension=0, tiled=True),
            lax.psum_scatter(gradients[3], "fsdp", scatter_dimension=0, tiled=True),
        )
    )


def micro_step(
    dec_rows, enc_rows, seg_rows_dec, seg_rows_enc, grad_rows, get_self, get_cross, get_ffn
):
    position = jnp.arange(seg_rows_dec.shape[1])
    causal = position[:, None] >= position[None, :]
    self_ok = (seg_rows_dec[:, :, None] == seg_rows_dec[:, None, :]) & causal[None]
    cross_ok = seg_rows_dec[:, :, None] == seg_rows_enc[:, None, :]
    gain_a, wq_a, wk_a, wv_a, wo_a = get_self()
    dec_float = dec_rows.astype(jnp.float32)
    normed_a = rms_forward(dec_float, gain_a.astype(jnp.float32)).astype(jnp.bfloat16)
    query_a = project(normed_a, wq_a).astype(jnp.bfloat16)
    keys_a = project(normed_a, wk_a).astype(jnp.bfloat16)
    values_a = project(normed_a, wv_a).astype(jnp.bfloat16)
    mix_a, total_a = attend_forward(query_a, keys_a, values_a, self_ok)
    after_self = dec_float + project(mix_a, wo_a)
    gain_c, wq_c, wk_c, wv_c, wo_c = get_cross()
    normed_c = rms_forward(after_self, gain_c.astype(jnp.float32)).astype(jnp.bfloat16)
    query_c = project(normed_c, wq_c).astype(jnp.bfloat16)
    keys_c = project(enc_rows, wk_c).astype(jnp.bfloat16)
    values_c = project(enc_rows, wv_c).astype(jnp.bfloat16)
    mix_c, total_c = attend_forward(query_c, keys_c, values_c, cross_ok)
    after_cross = after_self + project(mix_c, wo_c)
    gain_f, gate_w, up_w, down_w = get_ffn()
    normed_f = rms_forward(after_cross, gain_f.astype(jnp.float32)).astype(jnp.bfloat16)
    gate_pre = project(normed_f, gate_w)
    up_pre = project(normed_f, up_w)
    hidden_low = (jax.nn.gelu(gate_pre, approximate=True) * up_pre).astype(jnp.bfloat16)
    dec_result = (after_cross + project(hidden_low, down_w)).astype(jnp.bfloat16)
    gain_f, gate_w, up_w, down_w = get_ffn()
    grad_res = grad_rows.astype(jnp.float32)
    grad_branch = grad_res.astype(jnp.bfloat16)
    grad_down = weight_grad(hidden_low, grad_branch)
    grad_hidden = input_grad(grad_branch, down_w)
    _, gelu_pull = jax.vjp(
        lambda gate_in, up_in: jax.nn.gelu(gate_in, approximate=True) * up_in, gate_pre, up_pre
    )
    grad_gate_pre, grad_up_pre = gelu_pull(grad_hidden)
    grad_gate_low = grad_gate_pre.astype(jnp.bfloat16)
    grad_up_low = grad_up_pre.astype(jnp.bfloat16)
    grad_gate = weight_grad(normed_f, grad_gate_low)
    grad_up = weight_grad(normed_f, grad_up_low)
    grad_normed = input_grad(grad_gate_low, gate_w) + input_grad(grad_up_low, up_w)
    grad_input, grad_gain_f = rms_backward(after_cross, gain_f, grad_normed)
    grad_res = grad_res + grad_input
    gain_c, wq_c, wk_c, wv_c, wo_c = get_cross()
    grad_branch = grad_res.astype(jnp.bfloat16)
    grad_wo_c = weight_grad(mix_c, grad_branch)
    grad_mix = input_grad(grad_branch, wo_c).astype(jnp.bfloat16)
    grad_query, grad_keys, grad_values = attend_backward(
        query_c, keys_c, values_c, cross_ok, total_c, grad_mix
    )
    grad_wq_c = weight_grad(normed_c, grad_query)
    grad_wk_c = weight_grad(enc_rows, grad_keys)
    grad_wv_c = weight_grad(enc_rows, grad_values)
    grad_enc_rows = input_grad(grad_keys, wk_c) + input_grad(grad_values, wv_c)
    grad_normed = input_grad(grad_query, wq_c)
    grad_input, grad_gain_c = rms_backward(after_self, gain_c, grad_normed)
    grad_res = grad_res + grad_input
    gain_a, wq_a, wk_a, wv_a, wo_a = get_self()
    grad_branch = grad_res.astype(jnp.bfloat16)
    grad_wo_a = weight_grad(mix_a, grad_branch)
    grad_mix = input_grad(grad_branch, wo_a).astype(jnp.bfloat16)
    grad_query, grad_keys, grad_values = attend_backward(
        query_a, keys_a, values_a, self_ok, total_a, grad_mix
    )
    grad_wq_a = weight_grad(normed_a, grad_query)
    grad_wk_a = weight_grad(normed_a, grad_keys)
    grad_wv_a = weight_grad(normed_a, grad_values)
    grad_normed = (
        input_grad(grad_query, wq_a) + input_grad(grad_keys, wk_a) + input_grad(grad_values, wv_a)
    )
    grad_input, grad_gain_a = rms_backward(dec_float, gain_a, grad_normed)
    grad_dec_rows = grad_res + grad_input
    full_grads = (
        grad_gain_a,
        grad_wq_a,
        grad_wk_a,
        grad_wv_a,
        grad_wo_a,
        grad_gain_c,
        grad_wq_c,
        grad_wk_c,
        grad_wv_c,
        grad_wo_c,
        grad_gain_f,
        grad_gate,
        grad_up,
        grad_down,
    )
    return (dec_result, grad_dec_rows, grad_enc_rows, full_grads)


def body(
    dec_in,
    enc_out,
    seg_dec,
    seg_enc,
    out_grad,
    gain_self,
    wq_self,
    wk_self,
    wv_self,
    wo_self,
    gain_cross,
    wq_cross,
    wk_cross,
    wv_cross,
    wo_cross,
    gain_ffn,
    w_gate,
    w_up,
    w_down,
):
    get_self = lambda: fetch_self(gain_self, wq_self, wk_self, wv_self, wo_self)
    get_cross = lambda: fetch_cross(gain_cross, wq_cross, wk_cross, wv_cross, wo_cross)
    get_ffn = lambda: fetch_ffn(gain_ffn, w_gate, w_up, w_down)
    rows_micro = dec_in.shape[0] // MICRO
    outputs_dec = []
    grads_dec = []
    grads_enc = []
    gathered_sum = None
    for micro_index in range(MICRO):
        first_row = micro_index * rows_micro
        last_row = first_row + rows_micro
        result_rows, grad_rows_dec, grad_rows_enc, full_grads = micro_step(
            dec_in[first_row:last_row],
            enc_out[first_row:last_row],
            seg_dec[first_row:last_row],
            seg_enc[first_row:last_row],
            out_grad[first_row:last_row],
            get_self,
            get_cross,
            get_ffn,
        )
        outputs_dec.append(result_rows)
        grads_dec.append(grad_rows_dec)
        grads_enc.append(grad_rows_enc)
        new_terms = (
            share_self(full_grads[0:5])
            + share_cross(full_grads[5:10])
            + share_ffn(full_grads[10:14])
        )
        if gathered_sum is None:
            gathered_sum = new_terms
        else:
            gathered_sum = tuple(
                (earlier + latest for earlier, latest in zip(gathered_sum, new_terms))
            )
    quarters = (
        lax.psum_scatter(
            gathered_sum[0].astype(jnp.bfloat16), "dp", scatter_dimension=0, tiled=True
        ).astype(jnp.float32),
        lax.psum_scatter(
            gathered_sum[1].astype(jnp.bfloat16), "dp", scatter_dimension=0, tiled=True
        ).astype(jnp.float32),
        lax.psum_scatter(
            gathered_sum[2].astype(jnp.bfloat16), "dp", scatter_dimension=0, tiled=True
        ).astype(jnp.float32),
        lax.psum_scatter(
            gathered_sum[3].astype(jnp.bfloat16), "dp", scatter_dimension=0, tiled=True
        ).astype(jnp.float32),
        lax.psum_scatter(
            gathered_sum[4].astype(jnp.bfloat16), "dp", scatter_dimension=0, tiled=True
        ).astype(jnp.float32),
        lax.psum_scatter(
            gathered_sum[5].astype(jnp.bfloat16), "dp", scatter_dimension=0, tiled=True
        ).astype(jnp.float32),
        lax.psum_scatter(
            gathered_sum[6].astype(jnp.bfloat16), "dp", scatter_dimension=0, tiled=True
        ).astype(jnp.float32),
        lax.psum_scatter(
            gathered_sum[7].astype(jnp.bfloat16), "dp", scatter_dimension=0, tiled=True
        ).astype(jnp.float32),
        lax.psum_scatter(
            gathered_sum[8].astype(jnp.bfloat16), "dp", scatter_dimension=0, tiled=True
        ).astype(jnp.float32),
        lax.psum_scatter(
            gathered_sum[9].astype(jnp.bfloat16), "dp", scatter_dimension=0, tiled=True
        ).astype(jnp.float32),
        lax.psum_scatter(
            gathered_sum[10].astype(jnp.bfloat16), "dp", scatter_dimension=0, tiled=True
        ).astype(jnp.float32),
        lax.psum_scatter(
            gathered_sum[11].astype(jnp.bfloat16), "dp", scatter_dimension=0, tiled=True
        ).astype(jnp.float32),
        lax.psum_scatter(
            gathered_sum[12].astype(jnp.bfloat16), "dp", scatter_dimension=0, tiled=True
        ).astype(jnp.float32),
        lax.psum_scatter(
            gathered_sum[13].astype(jnp.bfloat16), "dp", scatter_dimension=0, tiled=True
        ).astype(jnp.float32),
    )
    summed = (
        lax.all_gather(quarters[0].astype(jnp.bfloat16), "dp", axis=0, tiled=True).astype(
            jnp.float32
        ),
        lax.all_gather(quarters[1].astype(jnp.bfloat16), "dp", axis=0, tiled=True).astype(
            jnp.float32
        ),
        lax.all_gather(quarters[2].astype(jnp.bfloat16), "dp", axis=0, tiled=True).astype(
            jnp.float32
        ),
        lax.all_gather(quarters[3].astype(jnp.bfloat16), "dp", axis=0, tiled=True).astype(
            jnp.float32
        ),
        lax.all_gather(quarters[4].astype(jnp.bfloat16), "dp", axis=0, tiled=True).astype(
            jnp.float32
        ),
        lax.all_gather(quarters[5].astype(jnp.bfloat16), "dp", axis=0, tiled=True).astype(
            jnp.float32
        ),
        lax.all_gather(quarters[6].astype(jnp.bfloat16), "dp", axis=0, tiled=True).astype(
            jnp.float32
        ),
        lax.all_gather(quarters[7].astype(jnp.bfloat16), "dp", axis=0, tiled=True).astype(
            jnp.float32
        ),
        lax.all_gather(quarters[8].astype(jnp.bfloat16), "dp", axis=0, tiled=True).astype(
            jnp.float32
        ),
        lax.all_gather(quarters[9].astype(jnp.bfloat16), "dp", axis=0, tiled=True).astype(
            jnp.float32
        ),
        lax.all_gather(quarters[10].astype(jnp.bfloat16), "dp", axis=0, tiled=True).astype(
            jnp.float32
        ),
        lax.all_gather(quarters[11].astype(jnp.bfloat16), "dp", axis=0, tiled=True).astype(
            jnp.float32
        ),
        lax.all_gather(quarters[12].astype(jnp.bfloat16), "dp", axis=0, tiled=True).astype(
            jnp.float32
        ),
        lax.all_gather(quarters[13].astype(jnp.bfloat16), "dp", axis=0, tiled=True).astype(
            jnp.float32
        ),
    )
    return (
        jnp.concatenate(outputs_dec, axis=0),
        jnp.concatenate(grads_dec, axis=0),
        jnp.concatenate(grads_enc, axis=0),
    ) + tuple(summed)


def solution(mesh):
    placed = (
        P(("dp", "fsdp"), None, None),
        P(("dp", "fsdp"), None, None),
        P(("dp", "fsdp"), None),
        P(("dp", "fsdp"), None),
        P(("dp", "fsdp"), None, None),
        P("fsdp"),
        P("fsdp", None),
        P("fsdp", None),
        P("fsdp", None),
        P("fsdp", None),
        P("fsdp"),
        P("fsdp", None),
        P("fsdp", None),
        P("fsdp", None),
        P("fsdp", None),
        P("fsdp"),
        P("fsdp", None),
        P("fsdp", None),
        P("fsdp", None),
    )
    return jax.shard_map(
        body,
        mesh=mesh,
        in_specs=placed,
        out_specs=(
            P(("dp", "fsdp"), None, None),
            P(("dp", "fsdp"), None, None),
            P(("dp", "fsdp"), None, None),
            P("fsdp"),
            P("fsdp", None),
            P("fsdp", None),
            P("fsdp", None),
            P("fsdp", None),
            P("fsdp"),
            P("fsdp", None),
            P("fsdp", None),
            P("fsdp", None),
            P("fsdp", None),
            P("fsdp"),
            P("fsdp", None),
            P("fsdp", None),
            P("fsdp", None),
        ),
        check_vma=False,
    )
```

profile of v0, /device:TPU:0, one launch (start us, length us, event | category | flops | bytes accessed | tf_op | source)
XLA Modules:
  0.0 1196.9 jit_solution(6850755473182431177)
XLA Ops:
  17.1 15.5 %all-reduce.13 = (bf16[768]{0:T(1024)(128)(2,1)S(1)}, bf16[768]{0:T(1024)(128)(2,1)S(1)}, bf16[768]{0:T(1024)(128)(2,1)S(1)}) all-reduce(bf16[768]{0:T(1024)(128)(2,1)S(1)} %dynamic-update-slice, bf16[768]{0:T(1024)(128)(2,1)S(1)} %dynamic-update-slice.1, bf16[768]{0:T(1024)(128)(2,1)S(1)} %dynamic-update-slice.2), channel_id=1, replica_groups=mesh['dp'=4,'fsdp'=8] {'fsdp'}, use_global_device_ids=true, to_apply=%add | all-reduce | flops 2304 | bytes 9216
  39.6 23.3 %all-gather.14.cloned.1.call-done = bf16[768,768]{1,0:T(8,128)(2,1)} async-done(((bf16[96,768]{1,0:T(8,128)(2,1)}), bf16[768,768]{1,0:T(8,128)(2,1)}) %all-gather.14.cloned.1.call-update) | async-done | bytes 1179664 | tf_op jit(solution)/shard_map/all_gather | solution.py:100
  64.8 24.1 %all-gather.16.cloned.1.call-done = bf16[768,768]{1,0:T(8,128)(2,1)} async-done(((bf16[96,768]{1,0:T(8,128)(2,1)}), bf16[768,768]{1,0:T(8,128)(2,1)}) %all-gather.16.cloned.1.call-update) | async-done | bytes 1179664 | tf_op jit(solution)/shard_map/all_gather | solution.py:101
  93.6 21.1 %all-gather.20.cloned.1.call-done = bf16[768,768]{1,0:T(8,128)(2,1)} async-done(((bf16[96,768]{1,0:T(8,128)(2,1)}), bf16[768,768]{1,0:T(8,128)(2,1)}) %all-gather.20.cloned.1.call-update) | async-done | bytes 1179664 | tf_op jit(solution)/shard_map/all_gather | solution.py:112
  121.6 18.9 %all-gather.18.cloned.1.call-done = bf16[768,768]{1,0:T(8,128)(2,1)} async-done(((bf16[96,768]{1,0:T(8,128)(2,1)}), bf16[768,768]{1,0:T(8,128)(2,1)}) %all-gather.18.cloned.1.call-update) | async-done | bytes 1179664 | tf_op jit(solution)/shard_map/all_gather | solution.py:103
  142.6 23.8 %all-gather.22.cloned.1.call-done = bf16[768,768]{1,0:T(8,128)(2,1)} async-done(((bf16[96,768]{1,0:T(8,128)(2,1)}), bf16[768,768]{1,0:T(8,128)(2,1)}) %all-gather.22.cloned.1.call-update) | async-done | bytes 1179664 | tf_op jit(solution)/shard_map/all_gather | solution.py:110
  169.0 23.3 %all-gather.24.cloned.1.call-done = bf16[768,768]{1,0:T(8,128)(2,1)} async-done(((bf16[96,768]{1,0:T(8,128)(2,1)}), bf16[768,768]{1,0:T(8,128)(2,1)}) %all-gather.24.cloned.1.call-update) | async-done | bytes 1179664 | tf_op jit(solution)/shard_map/all_gather | solution.py:111
  233.4 19.2 %all-gather.28.cloned.1.call-done = bf16[768,2048]{1,0:T(8,128)(2,1)} async-done(((bf16[96,2048]{1,0:T(8,128)(2,1)}), bf16[768,2048]{1,0:T(8,128)(2,1)}) %all-gather.28.cloned.1.call-update) | async-done | bytes 3145744 | tf_op jit(solution)/shard_map/all_gather | solution.py:120
  256.3 30.4 %all-gather.30.cloned.1.call-done = bf16[768,2048]{1,0:T(8,128)(2,1)} async-done(((bf16[96,2048]{1,0:T(8,128)(2,1)}), bf16[768,2048]{1,0:T(8,128)(2,1)}) %all-gather.30.cloned.1.call-update) | async-done | bytes 3145744 | tf_op jit(solution)/shard_map/all_gather | solution.py:121
  290.5 30.4 %all-gather.32.cloned.1.call-done = bf16[2048,768]{1,0:T(8,128)(2,1)} async-done(((bf16[256,768]{1,0:T(8,128)(2,1)}), bf16[2048,768]{1,0:T(8,128)(2,1)}) %all-gather.32.cloned.1.call-update) | async-done | bytes 3145744 | tf_op jit(solution)/shard_map/all_gather | solution.py:122
  452.7 21.7 %reduce-scatter.51.cloned.1.call-done = f32[96,768]{1,0:T(8,128)} async-done(((f32[768,768]{1,0:T(8,128)}), f32[96,768]{1,0:T(8,128)}) %reduce-scatter.51.cloned.1.call-update) | async-done | bytes 294928 | tf_op jit(solution)/shard_map/reduce_scatter | solution.py:131
  478.2 42.0 %reduce-scatter.53.cloned.1.call-done = f32[96,768]{1,0:T(8,128)} async-done(((f32[768,768]{1,0:T(8,128)}), f32[96,768]{1,0:T(8,128)}) %reduce-scatter.53.cloned.1.call-update) | async-done | bytes 294928 | tf_op jit(solution)/shard_map/reduce_scatter | solution.py:132
  524.4 41.9 %reduce-scatter.55.cloned.1.call-done = f32[96,768]{1,0:T(8,128)} async-done(((f32[768,768]{1,0:T(8,128)}), f32[96,768]{1,0:T(8,128)}) %reduce-scatter.55.cloned.1.call-update) | async-done | bytes 294928 | tf_op jit(solution)/shard_map/reduce_scatter | solution.py:133
  571.5 40.5 %reduce-scatter.57.cloned.1.call-done = f32[96,768]{1,0:T(8,128)} async-done(((f32[768,768]{1,0:T(8,128)}), f32[96,768]{1,0:T(8,128)}) %reduce-scatter.57.cloned.1.call-update) | async-done | bytes 294928 | tf_op jit(solution)/shard_map/reduce_scatter | solution.py:142
  618.9 39.1 %reduce-scatter.71.cloned.1.call-done = f32[96,768]{1,0:T(8,128)} async-done(((f32[768,768]{1,0:T(8,128)}), f32[96,768]{1,0:T(8,128)}) %reduce-scatter.71.cloned.1.call-update) | async-done | bytes 294928
  663.3 40.5 %reduce-scatter.73.cloned.1.call-done = f32[96,768]{1,0:T(8,128)} async-done(((f32[768,768]{1,0:T(8,128)}), f32[96,768]{1,0:T(8,128)}) %reduce-scatter.73.cloned.1.call-update) | async-done | bytes 294928
  710.4 39.7 %reduce-scatter.59.cloned.1.call-done = f32[96,768]{1,0:T(8,128)} async-done(((f32[768,768]{1,0:T(8,128)}), f32[96,768]{1,0:T(8,128)}) %reduce-scatter.59.cloned.1.call-update) | async-done | bytes 294928 | tf_op jit(solution)/shard_map/reduce_scatter | solution.py:145
  755.0 60.1 %reduce-scatter.61.cloned.1.call-done = f32[96,2048]{1,0:T(8,128)} async-done(((f32[768,2048]{1,0:T(8,128)}), f32[96,2048]{1,0:T(8,128)}) %reduce-scatter.61.cloned.1.call-update) | async-done | bytes 786448 | tf_op jit(solution)/shard_map/reduce_scatter | solution.py:154
  820.9 59.6 %reduce-scatter.63.cloned.1.call-done = f32[96,2048]{1,0:T(8,128)} async-done(((f32[768,2048]{1,0:T(8,128)}), f32[96,2048]{1,0:T(8,128)}) %reduce-scatter.63.cloned.1.call-update) | async-done | bytes 786448 | tf_op jit(solution)/shard_map/reduce_scatter | solution.py:155
  887.6 58.2 %reduce-scatter.65.cloned.1.call-done = f32[256,768]{1,0:T(8,128)} async-done(((f32[2048,768]{1,0:T(8,128)}), f32[256,768]{1,0:T(8,128)}) %reduce-scatter.65.cloned.1.call-update) | async-done | bytes 786448 | tf_op jit(solution)/shard_map/reduce_scatter | solution.py:156
  948.6 23.1 %all-reduce.12 = (bf16[768]{0:T(1024)(128)(2,1)S(1)}, bf16[768]{0:T(1024)(128)(2,1)S(1)}, bf16[768]{0:T(1024)(128)(2,1)S(1)}) all-reduce(f32[768]{0:T(1024)S(1)} %add.386, f32[768]{0:T(1024)S(1)} %add.391, f32[768]{0:T(1024)S(1)} %add.396), channel_id=16, replica_groups=mesh['dp'=4,'fsdp'=8] {'fsdp'}, use_global_device_ids=true, to_apply=%region_25.26.clone | all-reduce | flops 2304 | bytes 13824
  994.9 13.7 %all_gather.141 = bf16[96,768]{1,0:T(8,128)(2,1)S(1)} all-gather(bf16[24,768]{1,0:T(8,128)(2,1)} %reduce-scatter.31.cloned.1.call-done), channel_id=1, replica_groups=mesh['dp'=4,'fsdp'=8] {'dp'}, dimensions={0}, use_global_device_ids=true | all-gather | bytes 184320 | tf_op jit(solution)/shard_map/all_gather | solution.py:357
  1009.4 13.8 %all_gather.142 = bf16[96,768]{1,0:T(8,128)(2,1)S(1)} all-gather(bf16[24,768]{1,0:T(8,128)(2,1)} %reduce-scatter.33.cloned.1.call-done), channel_id=1, replica_groups=mesh['dp'=4,'fsdp'=8] {'dp'}, dimensions={0}, use_global_device_ids=true | all-gather | bytes 184320 | tf_op jit(solution)/shard_map/all_gather | solution.py:360
  1023.9 13.6 %all_gather.143 = bf16[96,768]{1,0:T(8,128)(2,1)S(1)} all-gather(bf16[24,768]{1,0:T(8,128)(2,1)} %reduce-scatter.35.cloned.1.call-done), channel_id=1, replica_groups=mesh['dp'=4,'fsdp'=8] {'dp'}, dimensions={0}, use_global_device_ids=true | all-gather | bytes 184320 | tf_op jit(solution)/shard_map/all_gather | solution.py:363
  1038.3 13.8 %all_gather.144 = bf16[96,768]{1,0:T(8,128)(2,1)S(1)} all-gather(bf16[24,768]{1,0:T(8,128)(2,1)} %reduce-scatter.37.cloned.1.call-done), channel_id=1, replica_groups=mesh['dp'=4,'fsdp'=8] {'dp'}, dimensions={0}, use_global_device_ids=true | all-gather | bytes 184320 | tf_op jit(solution)/shard_map/all_gather | solution.py:366
  1052.8 14.2 %all_gather.146 = bf16[96,768]{1,0:T(8,128)(2,1)S(1)} all-gather(bf16[24,768]{1,0:T(8,128)(2,1)} %reduce-scatter.39.cloned.1.call-done), channel_id=1, replica_groups=mesh['dp'=4,'fsdp'=8] {'dp'}, dimensions={0}, use_global_device_ids=true | all-gather | bytes 184320 | tf_op jit(solution)/shard_map/all_gather | solution.py:372
  1068.6 13.8 %all_gather.147 = bf16[96,768]{1,0:T(8,128)(2,1)S(1)} all-gather(bf16[24,768]{1,0:T(8,128)(2,1)} %reduce-scatter.67.cloned.1.call-done), channel_id=1, replica_groups=mesh['dp'=4,'fsdp'=8] {'dp'}, dimensions={0}, use_global_device_ids=true | all-gather | bytes 184320 | tf_op jit(solution)/shard_map/all_gather | solution.py:375
  1088.4 13.9 %all_gather.148 = bf16[96,768]{1,0:T(8,128)(2,1)S(1)} all-gather(bf16[24,768]{1,0:T(8,128)(2,1)} %reduce-scatter.69.cloned.1.call-done), channel_id=1, replica_groups=mesh['dp'=4,'fsdp'=8] {'dp'}, dimensions={0}, use_global_device_ids=true | all-gather | bytes 184320 | tf_op jit(solution)/shard_map/all_gather | solution.py:378
  1107.9 14.2 %all_gather.149 = bf16[96,768]{1,0:T(8,128)(2,1)S(1)} all-gather(bf16[24,768]{1,0:T(8,128)(2,1)} %reduce-scatter.41.cloned.1.call-done), channel_id=1, replica_groups=mesh['dp'=4,'fsdp'=8] {'dp'}, dimensions={0}, use_global_device_ids=true | all-gather | bytes 184320 | tf_op jit(solution)/shard_map/all_gather | solution.py:381
  1129.6 16.7 %all_gather.151 = bf16[96,2048]{1,0:T(8,128)(2,1)S(1)} all-gather(bf16[24,2048]{1,0:T(8,128)(2,1)} %reduce-scatter.43.cloned.1.call-done), channel_id=1, replica_groups=mesh['dp'=4,'fsdp'=8] {'dp'}, dimensions={0}, use_global_device_ids=true | all-gather | bytes 491520 | tf_op jit(solution)/shard_map/all_gather | solution.py:387
  1151.3 17.4 %all_gather.152 = bf16[96,2048]{1,0:T(8,128)(2,1)S(1)} all-gather(bf16[24,2048]{1,0:T(8,128)(2,1)} %reduce-scatter.45.cloned.1.call-done), channel_id=1, replica_groups=mesh['dp'=4,'fsdp'=8] {'dp'}, dimensions={0}, use_global_device_ids=true | all-gather | bytes 491520 | tf_op jit(solution)/shard_map/all_gather | solution.py:390
  1173.7 15.2 %all_gather.153 = bf16[256,768]{1,0:T(8,128)(2,1)S(1)} all-gather(bf16[64,768]{1,0:T(8,128)(2,1)} %reduce-scatter.47.cloned.1.call-done), channel_id=1, replica_groups=mesh['dp'=4,'fsdp'=8] {'dp'}, dimensions={0}, use_global_device_ids=true | all-gather | bytes 491520 | tf_op jit(solution)/shard_map/all_gather | solution.py:393
  (646 shorter events, 320.5 us)
Async XLA Ops:
  8.0 54.9 %all-gather.14.cloned.1.call-start = ((), (), s32[]{:S(2)}) async-start(), calls=%async_computation.23 | async-start | bytes 1327104 | tf_op jit(solution)/shard_map/all_gather | solution.py:100
  8.8 80.1 %all-gather.16.cloned.1.call-start = ((), (), s32[]{:S(2)}) async-start(), calls=%async_computation.24 | async-start | bytes 1327104 | tf_op jit(solution)/shard_map/all_gather | solution.py:101
  9.5 105.2 %all-gather.20.cloned.1.call-start = ((), (), s32[]{:S(2)}) async-start(), calls=%async_computation.26 | async-start | bytes 1327104 | tf_op jit(solution)/shard_map/all_gather | solution.py:112
  10.1 130.5 %all-gather.18.cloned.1.call-start = ((), (), s32[]{:S(2)}) async-start(), calls=%async_computation.25 | async-start | bytes 1327104 | tf_op jit(solution)/shard_map/all_gather | solution.py:103
  10.7 155.7 %all-gather.22.cloned.1.call-start = ((), (), s32[]{:S(2)}) async-start(), calls=%async_computation.27 | async-start | bytes 1327104 | tf_op jit(solution)/shard_map/all_gather | solution.py:110
  11.2 181.1 %all-gather.24.cloned.1.call-start = ((), (), s32[]{:S(2)}) async-start(), calls=%async_computation.28 | async-start | bytes 1327104 | tf_op jit(solution)/shard_map/all_gather | solution.py:111
  12.0 213.6 %all-gather.26.cloned.1.call-start = ((), (), s32[]{:S(2)}) async-start(), calls=%async_computation.29 | async-start | bytes 1327104 | tf_op jit(solution)/shard_map/all_gather | solution.py:113
  12.7 239.8 %all-gather.28.cloned.1.call-start = ((), (), s32[]{:S(2)}) async-start(), calls=%async_computation.30 | async-start | bytes 3538944 | tf_op jit(solution)/shard_map/all_gather | solution.py:120
  13.5 273.2 %all-gather.30.cloned.1.call-start = ((), (), s32[]{:S(2)}) async-start(), calls=%async_computation.31 | async-start | bytes 3538944 | tf_op jit(solution)/shard_map/all_gather | solution.py:121
  14.1 306.8 %all-gather.32.cloned.1.call-start = ((), (), s32[]{:S(2)}) async-start(), calls=%async_computation.32 | async-start | bytes 3538944 | tf_op jit(solution)/shard_map/all_gather | solution.py:122
  14.8 434.2 %reduce-scatter.49.cloned.1.call-start = ((), (), s32[]{:S(2)}) async-start(), calls=%async_computation.42 | async-start | bytes 2654208 | tf_op jit(solution)/shard_map/reduce_scatter | solution.py:130
  385.6 88.9 %reduce-scatter.51.cloned.1.call-start = ((), (), s32[]{:S(2)}) async-start(), calls=%async_computation.43 | async-start | bytes 2654208 | tf_op jit(solution)/shard_map/reduce_scatter | solution.py:131
  392.8 127.4 %reduce-scatter.53.cloned.1.call-start = ((), (), s32[]{:S(2)}) async-start(), calls=%async_computation.44 | async-start | bytes 2654208 | tf_op jit(solution)/shard_map/reduce_scatter | solution.py:132
  398.8 167.5 %reduce-scatter.55.cloned.1.call-start = ((), (), s32[]{:S(2)}) async-start(), calls=%async_computation.45 | async-start | bytes 2654208 | tf_op jit(solution)/shard_map/reduce_scatter | solution.py:133
  402.3 209.7 %reduce-scatter.57.cloned.1.call-start = ((), (), s32[]{:S(2)}) async-start(), calls=%async_computation.46 | async-start | bytes 2654208 | tf_op jit(solution)/shard_map/reduce_scatter | solution.py:142
  405.9 252.2 %reduce-scatter.71.cloned.1.call-start = ((), (), s32[]{:S(2)}) async-start(), calls=%async_computation.53 | async-start | bytes 2654208
  415.1 288.7 %reduce-scatter.73.cloned.1.call-start = ((), (), s32[]{:S(2)}) async-start(), calls=%async_computation.54 | async-start | bytes 2654208
  427.6 322.4 %reduce-scatter.59.cloned.1.call-start = ((), (), s32[]{:S(2)}) async-start(), calls=%async_computation.47 | async-start | bytes 2654208 | tf_op jit(solution)/shard_map/reduce_scatter | solution.py:145
  431.1 384.0 %reduce-scatter.61.cloned.1.call-start = ((), (), s32[]{:S(2)}) async-start(), calls=%async_computation.48 | async-start | bytes 7077888 | tf_op jit(solution)/shard_map/reduce_scatter | solution.py:154
  436.8 443.7 %reduce-scatter.63.cloned.1.call-start = ((), (), s32[]{:S(2)}) async-start(), calls=%async_computation.49 | async-start | bytes 7077888 | tf_op jit(solution)/shard_map/reduce_scatter | solution.py:155
  442.8 503.0 %reduce-scatter.65.cloned.1.call-start = ((), (), s32[]{:S(2)}) async-start(), calls=%async_computation.50 | async-start | bytes 7077888 | tf_op jit(solution)/shard_map/reduce_scatter | solution.py:156
  448.9 546.0 %reduce-scatter.31.cloned.1.call-start = ((), (), s32[]{:S(2)}) async-start(), calls=%async_computation.33 | async-start | bytes 184320 | tf_op jit(solution)/shard_map/reduce_scatter | solution.py:313
  450.8 558.7 %reduce-scatter.33.cloned.1.call-start = ((), (), s32[]{:S(2)}) async-start(), calls=%async_computation.34 | async-start | bytes 184320 | tf_op jit(solution)/shard_map/reduce_scatter | solution.py:316
  476.1 547.8 %reduce-scatter.35.cloned.1.call-start = ((), (), s32[]{:S(2)}) async-start(), calls=%async_computation.35 | async-start | bytes 184320 | tf_op jit(solution)/shard_map/reduce_scatter | solution.py:319
  521.9 516.4 %reduce-scatter.37.cloned.1.call-start = ((), (), s32[]{:S(2)}) async-start(), calls=%async_computation.36 | async-start | bytes 184320 | tf_op jit(solution)/shard_map/reduce_scatter | solution.py:322
  567.9 484.9 %reduce-scatter.39.cloned.1.call-start = ((), (), s32[]{:S(2)}) async-start(), calls=%async_computation.37 | async-start | bytes 184320 | tf_op jit(solution)/shard_map/reduce_scatter | solution.py:328
  613.7 454.9 %reduce-scatter.67.cloned.1.call-start = ((), (), s32[]{:S(2)}) async-start(), calls=%async_computation.51 | async-start | bytes 184320 | tf_op jit(solution)/shard_map/reduce_scatter | solution.py:331
  660.0 428.4 %reduce-scatter.69.cloned.1.call-start = ((), (), s32[]{:S(2)}) async-start(), calls=%async_computation.52 | async-start | bytes 184320 | tf_op jit(solution)/shard_map/reduce_scatter | solution.py:334
  705.8 402.1 %reduce-scatter.41.cloned.1.call-start = ((), (), s32[]{:S(2)}) async-start(), calls=%async_computation.38 | async-start | bytes 184320 | tf_op jit(solution)/shard_map/reduce_scatter | solution.py:337
  751.7 377.9 %reduce-scatter.43.cloned.1.call-start = ((), (), s32[]{:S(2)}) async-start(), calls=%async_computation.39 | async-start | bytes 491520 | tf_op jit(solution)/shard_map/reduce_scatter | solution.py:343
  817.0 334.3 %reduce-scatter.45.cloned.1.call-start = ((), (), s32[]{:S(2)}) async-start(), calls=%async_computation.40 | async-start | bytes 491520 | tf_op jit(solution)/shard_map/reduce_scatter | solution.py:346
  882.5 291.2 %reduce-scatter.47.cloned.1.call-start = ((), (), s32[]{:S(2)}) async-start(), calls=%async_computation.41 | async-start | bytes 491520 | tf_op jit(solution)/shard_map/reduce_scatter | solution.py:349
  (183 other events, 2639.8 us)
Sparse Core Ops, SparseCore 0:
  10.0 26.9 all-gather.11
  38.9 23.9 all-gather.13
  64.8 24.0 all-gather.15
  90.6 24.0 all-gather.19
  116.4 24.0 all-gather.17
  142.3 24.0 all-gather.21
  168.2 24.0 all-gather.23
  194.2 24.0 all-gather.25
  220.2 32.2 all-gather.27
  254.3 32.3 all-gather.29
  288.5 32.3 all-gather.31
  385.7 42.4 reduce-scatter.48
  432.0 42.4 reduce-scatter.50
  477.7 42.4 reduce-scatter.52
  523.8 42.4 reduce-scatter.54
  569.5 42.4 reduce-scatter.56
  615.6 42.4 reduce-scatter.70
  661.3 42.4 reduce-scatter.72
  707.5 42.4 reduce-scatter.58
  753.3 61.7 reduce-scatter.60
  818.8 61.7 reduce-scatter.62
  883.9 61.7 reduce-scatter.64
  948.6 19.2 reduce-scatter.30
  970.6 17.4 reduce-scatter.32
  991.0 17.5 reduce-scatter.34
  1011.3 18.1 reduce-scatter.36
  1051.1 17.4 reduce-scatter.66
  1070.9 17.4 reduce-scatter.68
  1090.5 17.3 reduce-scatter.40
  1110.9 18.6 reduce-scatter.42
  1132.4 18.8 reduce-scatter.44
  1153.5 20.1 reduce-scatter.46
  (1 shorter events, 17.2 us)
where the time goes:
time: 1210 us; the launch traced here: 1200 us
  waiting for transfers between devices  694 us (57%)
  blocking collectives  220 us (18%)
  matrix products  161 us (13%)
  local copies, waits for them, and re-layouts  57.3 us (5%)
  other arithmetic  43.2 us (4%)
  between operations  19.8 us (2%)
    unnamed x35, waiting for transfers between devices  86.9 us
    reduce_scatter x1, waiting for transfers between devices, share_ffn(): lax.psum_scatter(gradients[1], 'fsdp', scatter_dimension=0, tiled=True)  60.1 us
    reduce_scatter x1, waiting for transfers between devices, share_ffn(): lax.psum_scatter(gradients[2], 'fsdp', scatter_dimension=0, tiled=True)  59.6 us
    unnamed x4, blocking collectives  59.3 us
    reduce_scatter x1, waiting for transfers between devices, share_ffn(): lax.psum_scatter(gradients[3], 'fsdp', scatter_dimension=0, tiled=True)  58.2 us
    dot_general x22, matrix products, input_grad(): jnp.einsum('rln,dn->rld', grad_out, weight, preferred_element_type=jnp.fl...  44.6 us
    reduce_scatter x1, waiting for transfers between devices, share_self(): lax.psum_scatter(gradients[3], 'fsdp', scatter_dimension=0, tiled=True)  42 us
    reduce_scatter x1, waiting for transfers between devices, share_self(): lax.psum_scatter(gradients[4], 'fsdp', scatter_dimension=0, tiled=True)  41.9 us
  transfers between devices with their start and end apart: 33, of which 26 were waited for; matrix products, arithmetic and copies ran while one was open for 15% of the time, Pallas kernels for 0%

commit v1 on v0

--- a/solution.py
+++ b/solution.py
@@ -4,7 +4,6 @@
 from jax.sharding import PartitionSpec as P
 
 HD = 64
-MICRO = 2
 
 
 EPSILON = 1e-06
@@ -94,68 +93,37 @@
     )
 
 
-def fetch_self(gain_vec, query_w, key_w, value_w, output_w):
-    return (
-        lax.all_gather(gain_vec, "fsdp", axis=0, tiled=True),
-        lax.all_gather(query_w, "fsdp", axis=0, tiled=True),
-        lax.all_gather(key_w, "fsdp", axis=0, tiled=True),
-        lax.all_gather(value_w, "fsdp", axis=0, tiled=True),
-        lax.all_gather(output_w, "fsdp", axis=0, tiled=True),
-    )
-
-
-def fetch_cross(gain_vec, query_w, key_w, value_w, output_w):
-    return (
-        lax.all_gather(gain_vec, "fsdp", axis=0, tiled=True),
-        lax.all_gather(query_w, "fsdp", axis=0, tiled=True),
-        lax.all_gather(key_w, "fsdp", axis=0, tiled=True),
-        lax.all_gather(value_w, "fsdp", axis=0, tiled=True),
-        lax.all_gather(output_w, "fsdp", axis=0, tiled=True),
-    )
-
-
-def fetch_ffn(gain_vec, gate_w, up_w, down_w):
-    return (
-        lax.all_gather(gain_vec, "fsdp", axis=0, tiled=True),
-        lax.all_gather(gate_w, "fsdp", axis=0, tiled=True),
-        lax.all_gather(up_w, "fsdp", axis=0, tiled=True),
-        lax.all_gather(down_w, "fsdp", axis=0, tiled=True),
-    )
-
-
-def share_self(gradients):
-    return tuple(
-        (
-            lax.psum_scatter(gradients[0], "fsdp", scatter_dimension=0, tiled=True),
-            lax.psum_scatter(gradients[1], "fsdp", scatter_dimension=0, tiled=True),
-            lax.psum_scatter(gradients[2], "fsdp", scatter_dimension=0, tiled=True),
-            lax.psum_scatter(gradients[3], "fsdp", scatter_dimension=0, tiled=True),
-            lax.psum_scatter(gradients[4], "fsdp", scatter_dimension=0, tiled=True),
-        )
-    )
-
-
-def share_cross(gradients):
-    return tuple(
-        (
-            lax.psum_scatter(gradients[0], "fsdp", scatter_dimension=0, tiled=True),
-            lax.psum_scatter(gradients[1], "fsdp", scatter_dimension=0, tiled=True),
-            lax.psum_scatter(gradients[2], "fsdp", scatter_dimension=0, tiled=True),
-            lax.psum_scatter(gradients[3], "fsdp", scatter_dimension=0, tiled=True),
-            lax.psum_scatter(gradients[4], "fsdp", scatter_dimension=0, tiled=True),
-        )
-    )
-
-
-def share_ffn(gradients):
-    return tuple(
-        (
-            lax.psum_scatter(gradients[0], "fsdp", scatter_dimension=0, tiled=True),
-            lax.psum_scatter(gradients[1], "fsdp", scatter_dimension=0, tiled=True),
-            lax.psum_scatter(gradients[2], "fsdp", scatter_dimension=0, tiled=True),
-            lax.psum_scatter(gradients[3], "fsdp", scatter_dimension=0, tiled=True),
-        )
-    )
+def gather_group(shards):
+    joined = jnp.concatenate(shards, axis=0)
+    whole = lax.all_gather(joined, "fsdp", axis=0, tiled=False)
+    parts = []
+    start = 0
+    for shard in shards:
+        part = whole[:, start : start + shard.shape[0]]
+        parts.append(part.reshape((-1,) + shard.shape[1:]))
+        start += shard.shape[0]
+    return parts
+
+
+def reduce_group(gradients, shards):
+    count = lax.axis_size("fsdp")
+    joined = jnp.concatenate(
+        [
+            gradient.astype(jnp.bfloat16).reshape((count, -1) + gradient.shape[1:])
+            for gradient in gradients
+        ],
+        axis=1,
+    )
+    owned = lax.psum_scatter(joined, "fsdp", scatter_dimension=0, tiled=False)
+    quarter = lax.psum_scatter(owned, "dp", scatter_dimension=0, tiled=True)
+    summed = lax.all_gather(quarter, "dp", axis=0, tiled=True)
+    parts = []
+    start = 0
+    for shard in shards:
+        part = summed[start : start + shard.shape[0]]
+        parts.append(part.astype(jnp.float32))
+        start += shard.shape[0]
+    return parts
 
 
 def micro_step(
@@ -271,134 +239,26 @@
     w_up,
     w_down,
 ):
-    get_self = lambda: fetch_self(gain_self, wq_self, wk_self, wv_self, wo_self)
-    get_cross = lambda: fetch_cross(gain_cross, wq_cross, wk_cross, wv_cross, wo_cross)
-    get_ffn = lambda: fetch_ffn(gain_ffn, w_gate, w_up, w_down)
-    rows_micro = dec_in.shape[0] // MICRO
-    outputs_dec = []
-    grads_dec = []
-    grads_enc = []
-    gathered_sum = None
-    for micro_index in range(MICRO):
-        first_row = micro_index * rows_micro
-        last_row = first_row + rows_micro
-        result_rows, grad_rows_dec, grad_rows_enc, full_grads = micro_step(
-            dec_in[first_row:last_row],
-            enc_out[first_row:last_row],
-            seg_dec[first_row:last_row],
-            seg_enc[first_row:last_row],
-            out_grad[first_row:last_row],
-            get_self,
-            get_cross,
-            get_ffn,
-        )
-        outputs_dec.append(result_rows)
-        grads_dec.append(grad_rows_dec)
-        grads_enc.append(grad_rows_enc)
-        new_terms = (
-            share_self(full_grads[0:5])
-            + share_cross(full_grads[5:10])
-            + share_ffn(full_grads[10:14])
-        )
-        if gathered_sum is None:
-            gathered_sum = new_terms
-        else:
-            gathered_sum = tuple(
-                (earlier + latest for earlier, latest in zip(gathered_sum, new_terms))
-            )
-    quarters = (
-        lax.psum_scatter(
-            gathered_sum[0].astype(jnp.bfloat16), "dp", scatter_dimension=0, tiled=True
-        ).astype(jnp.float32),
-        lax.psum_scatter(
-            gathered_sum[1].astype(jnp.bfloat16), "dp", scatter_dimension=0, tiled=True
-        ).astype(jnp.float32),
-        lax.psum_scatter(
-            gathered_sum[2].astype(jnp.bfloat16), "dp", scatter_dimension=0, tiled=True
-        ).astype(jnp.float32),
-        lax.psum_scatter(
-            gathered_sum[3].astype(jnp.bfloat16), "dp", scatter_dimension=0, tiled=True
-        ).astype(jnp.float32),
-        lax.psum_scatter(
-            gathered_sum[4].astype(jnp.bfloat16), "dp", scatter_dimension=0, tiled=True
-        ).astype(jnp.float32),
-        lax.psum_scatter(
-            gathered_sum[5].astype(jnp.bfloat16), "dp", scatter_dimension=0, tiled=True
-        ).astype(jnp.float32),
-        lax.psum_scatter(
-            gathered_sum[6].astype(jnp.bfloat16), "dp", scatter_dimension=0, tiled=True
-        ).astype(jnp.float32),
-        lax.psum_scatter(
-            gathered_sum[7].astype(jnp.bfloat16), "dp", scatter_dimension=0, tiled=True
-        ).astype(jnp.float32),
-        lax.psum_scatter(
-            gathered_sum[8].astype(jnp.bfloat16), "dp", scatter_dimension=0, tiled=True
-        ).astype(jnp.float32),
-        lax.psum_scatter(
-            gathered_sum[9].astype(jnp.bfloat16), "dp", scatter_dimension=0, tiled=True
-        ).astype(jnp.float32),
-        lax.psum_scatter(
-            gathered_sum[10].astype(jnp.bfloat16), "dp", scatter_dimension=0, tiled=True
-        ).astype(jnp.float32),
-        lax.psum_scatter(
-            gathered_sum[11].astype(jnp.bfloat16), "dp", scatter_dimension=0, tiled=True
-        ).astype(jnp.float32),
-        lax.psum_scatter(
-            gathered_sum[12].astype(jnp.bfloat16), "dp", scatter_dimension=0, tiled=True
-        ).astype(jnp.float32),
-        lax.psum_scatter(
-            gathered_sum[13].astype(jnp.bfloat16), "dp", scatter_dimension=0, tiled=True
-        ).astype(jnp.float32),
-    )
-    summed = (
-        lax.all_gather(quarters[0].astype(jnp.bfloat16), "dp", axis=0, tiled=True).astype(
-            jnp.float32
-        ),
-        lax.all_gather(quarters[1].astype(jnp.bfloat16), "dp", axis=0, tiled=True).astype(
-            jnp.float32
-        ),
-        lax.all_gather(quarters[2].astype(jnp.bfloat16), "dp", axis=0, tiled=True).astype(
-            jnp.float32
-        ),
-        lax.all_gather(quarters[3].astype(jnp.bfloat16), "dp", axis=0, tiled=True).astype(
-            jnp.float32
-        ),
-        lax.all_gather(quarters[4].astype(jnp.bfloat16), "dp", axis=0, tiled=True).astype(
-            jnp.float32
-        ),
-        lax.all_gather(quarters[5].astype(jnp.bfloat16), "dp", axis=0, tiled=True).astype(
-            jnp.float32
-        ),
-        lax.all_gather(quarters[6].astype(jnp.bfloat16), "dp", axis=0, tiled=True).astype(
-            jnp.float32
-        ),
-        lax.all_gather(quarters[7].astype(jnp.bfloat16), "dp", axis=0, tiled=True).astype(
-            jnp.float32
-        ),
-        lax.all_gather(quarters[8].astype(jnp.bfloat16), "dp", axis=0, tiled=True).astype(
-            jnp.float32
-        ),
-        lax.all_gather(quarters[9].astype(jnp.bfloat16), "dp", axis=0, tiled=True).astype(
-            jnp.float32
-        ),
-        lax.all_gather(quarters[10].astype(jnp.bfloat16), "dp", axis=0, tiled=True).astype(
-            jnp.float32
-        ),
-        lax.all_gather(quarters[11].astype(jnp.bfloat16), "dp", axis=0, tiled=True).astype(
-            jnp.float32
-        ),
-        lax.all_gather(quarters[12].astype(jnp.bfloat16), "dp", axis=0, tiled=True).astype(
-            jnp.float32
-        ),
-        lax.all_gather(quarters[13].astype(jnp.bfloat16), "dp", axis=0, tiled=True).astype(
-            jnp.float32
-        ),
-    )
+    narrow = (wq_self, wk_self, wv_self, wo_self, wq_cross, wk_cross, wv_cross, wo_cross, w_down)
+    gain_a, gain_c, gain_f = gather_group((gain_self, gain_cross, gain_ffn))
+    full = gather_group(narrow)
+    gate_full, up_full = gather_group((w_gate, w_up))
+    get_self = lambda: (gain_a, *full[0:4])
+    get_cross = lambda: (gain_c, *full[4:8])
+    get_ffn = lambda: (gain_f, gate_full, up_full, full[8])
+    result_rows, grad_rows_dec, grad_rows_enc, grads = micro_step(
+        dec_in, enc_out, seg_dec, seg_enc, out_grad, get_self, get_cross, get_ffn
+    )
+    gains = reduce_group((grads[0], grads[5], grads[10]), (gain_self, gain_cross, gain_ffn))
+    wide = reduce_group(grads[11:13], (w_gate, w_up))
+    thin = reduce_group(grads[1:5] + grads[6:10] + grads[13:14], narrow)
     return (
-        jnp.concatenate(outputs_dec, axis=0),
-        jnp.concatenate(grads_dec, axis=0),
-        jnp.concatenate(grads_enc, axis=0),
-    ) + tuple(summed)
+        (result_rows, grad_rows_dec, grad_rows_enc, gains[0])
+        + tuple(thin[0:4])
+        + (gains[1],)
+        + tuple(thin[4:8])
+        + (gains[2], *wide, thin[8])
+    )
 
 
 def solution(mesh):

time: 1210 us -> 549 us (0.45)
  waiting for transfers between devices: 694 us -> 267 us
  blocking collectives: 220 us -> 77.3 us
  matrix products: 161 us -> 98.7 us
  other arithmetic: 43.2 us -> 26.8 us
    reduce_scatter x20 -> x4, waiting for transfers between devices: 390 us -> 173 us  [the longest x2 146 us: reduce_group(): owned = lax.psum_scatter(joined, 'fsdp', scatter_dimension=0, tiled=False)]
    all_gather x11 -> x1, blocking collectives: 160 us -> 28.7 us  [reduce_group(): summed = lax.all_gather(quarter, 'dp', axis=0, tiled=True)]
    all_gather x11 -> x3, waiting for transfers between devices: 218 us -> 93.8 us  [the longest x2 91.4 us: gather_group(): whole = lax.all_gather(joined, 'fsdp', axis=0, tiled=False)]
    unnamed x35 -> x7, waiting for transfers between devices: 86.9 us -> 0.11 us
    dot_general x22 -> x11, matrix products: 41.1 us -> 20.7 us  [project(): jnp.einsum('rld,dn->rln', acts, weight, preferred_element_type=jnp.float32)]
    dot_general x22 -> x11, matrix products: 44.6 us -> 25.4 us  [input_grad(): jnp.einsum('rln,dn->rld', grad_out, weight, preferred_element_type=jnp.fl...]
    convert_element_type x25 -> x5, other arithmetic: 26 us -> 6.75 us  [the longest x4 6.59 us: reduce_group(): parts.append(part.astype(jnp.float32))]
    slice x2 -> x3, local copies, waits for them, and re-layouts: 0.01 us -> 17.4 us  [gather_group(): part = whole[:, start:start + shard.shape[0]]]
  transfers between devices with their start and end apart: 33 -> 7, of which waited for: 26 -> 6; matrix products, arithmetic and copies ran while one was open for 15% -> 8% of each run, Pallas kernels for 0% -> 0%
where the time goes in v1:
time: 549 us; the launch traced here: 545 us
  waiting for transfers between devices  267 us (49%)
  matrix products  98.7 us (18%)
  blocking collectives  77.3 us (14%)
  local copies, waits for them, and re-layouts  57.7 us (11%)
  other arithmetic  26.8 us (5%)
  between operations  17.4 us (3%)
    reduce_scatter x2, waiting for transfers between devices, reduce_group(): owned = lax.psum_scatter(joined, 'fsdp', scatter_dimension=0, tiled=False)  146 us
    all_gather x2, waiting for transfers between devices, gather_group(): whole = lax.all_gather(joined, 'fsdp', axis=0, tiled=False)  91.4 us
    unnamed x4, blocking collectives  48.6 us
    all_gather x1, blocking collectives, reduce_group(): summed = lax.all_gather(quarter, 'dp', axis=0, tiled=True)  28.7 us
    unnamed x198, local copies, waits for them, and re-layouts  26.9 us
    reduce_scatter x2, waiting for transfers between devices, reduce_group(): quarter = lax.psum_scatter(owned, 'dp', scatter_dimension=0, tiled=True)  26.7 us
    dot_general x11, matrix products, input_grad(): jnp.einsum('rln,dn->rld', grad_out, weight, preferred_element_type=jnp.fl...  25.4 us
    dot_general x11, matrix products, project(): jnp.einsum('rld,dn->rln', acts, weight, preferred_element_type=jnp.float32)  20.7 us
  transfers between devices with their start and end apart: 7, of which 6 were waited for; matrix products, arithmetic and copies ran while one was open for 8% of the time, Pallas kernels for 0%

profile of v1, /device:TPU:0, one launch (start us, length us, event | category | flops | bytes accessed | tf_op | source)
XLA Modules:
  0.0 545.3 jit_solution(10635128616492890739)
XLA Ops:
  17.5 16.0 %all-reduce = bf16[2304]{0:T(1024)(128)(2,1)S(1)} all-reduce(bf16[2304]{0:T(1024)(128)(2,1)S(1)} %dynamic-update-slice), channel_id=2, replica_groups=mesh['dp'=4,'fsdp'=8] {'fsdp'}, use_global_device_ids=true, to_apply=%add | all-reduce | flops 2304 | bytes 9216
  35.1 24.0 %all-gather.11.cloned.1.call-done = bf16[1536,2048]{1,0:T(8,128)(2,1)} async-done(((bf16[192,2048]{1,0:T(8,128)(2,1)}), bf16[1536,2048]{1,0:T(8,128)(2,1)}) %all-gather.11.cloned.1.call-update) | async-done | bytes 6291472 | tf_op jit(solution)/shard_map/all_gather | solution.py:98
  59.1 6.7 %fusion.43 = (bf16[8,96,2048]{2,1,0:T(8,128)(2,1)}, bf16[8,96,2048]{2,1,0:T(8,128)(2,1)}) fusion(bf16[8,192,2048]{2,1,0:T(8,128)(2,1)} %bitcast.212), kind=kLoop, calls=%fused_computation.149 | loop fusion | bytes 12582912 | tf_op jit(solution)/shard_map/slice | solution.py:102
  65.8 67.4 %all-gather.9.cloned.1.call-done = bf16[8192,768]{1,0:T(8,128)(2,1)} async-done(((bf16[1024,768]{1,0:T(8,128)(2,1)}), bf16[8192,768]{1,0:T(8,128)(2,1)}) %all-gather.9.cloned.1.call-update) | async-done | bytes 12582928 | tf_op jit(solution)/shard_map/all_gather | solution.py:98
  133.1 3.8 slice.125
  136.9 6.9 %fusion.42 = (bf16[8,96,768]{2,1,0:T(8,128)(2,1)}, bf16[8,96,768]{2,1,0:T(8,128)(2,1)}, bf16[8,96,768]{2,1,0:T(8,128)(2,1)}, bf16[8,96,768]{2,1,0:T(8,128)(2,1)}...) fusion(bf16[8,1024,768]{2,1,0:T(8,128)(2,1)} %bitcast.197), kind=kLoop, calls=%fused_computation.148 | loop fusion | bytes 18874368 | tf_op jit(solution)/shard_map/slice | solution.py:102
  145.8 2.7 convolution_convert_fusion.10
  149.8 3.2 convolution_convert_fusion.11
  155.2 3.9 convolution_convert_fusion.1
  159.2 2.6 convolution_convert_fusion.2
  171.3 3.5 fusion
  174.9 3.2 exponential_reduce_fusion
  178.3 2.6 convolution_convert_fusion.3
  187.1 4.7 multiply_convert_fusion.3
  201.5 7.2 %convolution_convert_fusion = bf16[2,12,64,512]{3,2,1,0:T(8,128)(2,1)} fusion(bf16[2,176,12,64]{1,3,2,0:T(8,128)(2,1)} %bitcast.225, f32[2,12,176,512]{3,2,1,0:T(8,128)} %copy-done.1, f32[2,12,176]{2,1,0:T(8,128)} %copy-done.55, pred[2,176,512]{2,1,0:T(8,128)(4,1)} %broadcast_compare_fusion), kind=kOutput, calls=%fused_computation.46 | convolution fusion | flops 286261248 | bytes 10961408 | tf_op jit(solution)/shard_map/rhqk,rqhd->rkhd/dot_general | solution.py:71
  208.7 5.9 %multiply_reduce_fusion = (f32[2,12,176]{2,1,0:T(8,128)S(1)}, f32[2,12,176,512]{3,2,1,0:T(8,128)S(1)}) fusion(f32[2,12,176,512]{3,2,1,0:T(8,128)} %copy-done.1, f32[2,12,176]{2,1,0:T(8,128)S(1)} %copy-done.56, pred[2,176,512]{2,1,0:T(8,128)(4,1)S(1)} %copy-done.30, bf16[2,176,12,64]{1,3,2,0:T(8,128)(2,1)S(1)} %bitcast.226, ...), kind=kOutput, calls=%fused_computation.1 | convolution fusion | flops 287633280 | bytes 19629056 | tf_op jit(solution)/shard_map/rqhd,rkhd->rhqk/dot_general | solution.py:77
  214.7 2.7 multiply_convert_fusion
  230.6 3.5 convolution_convert_fusion.4
  234.1 4.1 multiply_reduce_fusion.1
  263.9 3.3 bitcast_convert_fusion
  269.1 4.9 pad_maximum_fusion
  274.1 81.4 %reduce-scatter.5.cloned.1.call-done = bf16[1,1024,768]{2,1,0:T(8,128)(2,1)} async-done(((bf16[8,1024,768]{2,1,0:T(8,128)(2,1)}), bf16[1,1024,768]{2,1,0:T(8,128)(2,1)}) %reduce-scatter.5.cloned.1.call-update) | async-done | bytes 1572880 | tf_op jit(solution)/shard_map/reduce_scatter | solution.py:117
  355.5 64.9 %reduce-scatter.9.cloned.1.call-done = bf16[1,192,2048]{2,1,0:T(8,128)(2,1)} async-done(((bf16[8,192,2048]{2,1,0:T(8,128)(2,1)}), bf16[1,192,2048]{2,1,0:T(8,128)(2,1)}) %reduce-scatter.9.cloned.1.call-update) | async-done | bytes 786448 | tf_op jit(solution)/shard_map/reduce_scatter | solution.py:117
  428.8 2.5 fusion.18
  431.3 26.7 %reduce-scatter.7.cloned.1.call-done = bf16[256,768]{1,0:T(8,128)(2,1)} async-done(((bf16[1024,768]{1,0:T(8,128)(2,1)}), bf16[256,768]{1,0:T(8,128)(2,1)}) %reduce-scatter.7.cloned.1.call-update) | async-done | bytes 393232 | tf_op jit(solution)/shard_map/reduce_scatter | solution.py:118
  458.1 13.7 %all-reduce.2 = bf16[8,288]{1,0:T(8,128)(2,1)S(1)} all-reduce(bf16[8,288]{1,0:T(8,128)(2,1)S(1)} %pad_maximum_fusion.2), channel_id=5, replica_groups=mesh['dp'=4,'fsdp'=8] {'fsdp'}, use_global_device_ids=true, to_apply=%region_15.16.clone | all-reduce | flops 2304 | bytes 9216
  472.5 10.3 %all-reduce.3 = bf16[288]{0:T(512)(128)(2,1)S(1)} all-reduce(bf16[288]{0:T(512)(128)(2,1)S(1)} %dynamic-slice_reduce_fusion), channel_id=6, replica_groups=mesh['dp'=4,'fsdp'=8] {'dp'}, use_global_device_ids=true, to_apply=%region_16.17.clone | all-reduce | flops 288 | bytes 1152
  483.1 8.6 %all-reduce.1 = bf16[288]{0:T(512)(128)(2,1)S(1)} all-reduce(bf16[288]{0:T(512)(128)(2,1)S(1)} %dynamic-update-slice.1), channel_id=1, replica_groups=mesh['dp'=4,'fsdp'=8] {'dp'}, use_global_device_ids=true, to_apply=%add.1 | all-reduce | flops 288 | bytes 1152
  492.3 3.3 fusion.50
  497.9 3.1 convolution_add_fusion
  501.0 28.7 %all_gather.35 = bf16[192,2048]{1,0:T(8,128)(2,1)S(1)} all-gather(bf16[48,2048]{1,0:T(8,128)(2,1)} %reduce-scatter.11.cloned.1.call-done), channel_id=1, replica_groups=mesh['dp'=4,'fsdp'=8] {'dp'}, dimensions={0}, use_global_device_ids=true | all-gather | bytes 983040 | tf_op jit(solution)/shard_map/all_gather | solution.py:119
  535.4 2.8 slice_convert_fusion.3
  (287 shorter events, 99.1 us)
Async XLA Ops:
  7.2 148.0 %copy-start = (bf16[2,512,768]{2,1,0:T(8,128)(2,1)S(1)}, bf16[2,512,768]{2,1,0:T(8,128)(2,1)}, u32[]{:S(2)}) copy-start(bf16[2,512,768]{2,1,0:T(8,128)(2,1)} %param.20) | copy-start | bytes 4718596
  7.2 4.4 copy-start.60
  7.2 5.1 copy-start.61
  7.3 5.7 %copy-start.62 = (bf16[96,768]{1,0:T(8,128)(2,1)S(1)}, bf16[96,768]{1,0:T(8,128)(2,1)}, u32[]{:S(2)}) copy-start(bf16[96,768]{1,0:T(8,128)(2,1)} %param.31) | copy-start | bytes 442372
  7.3 51.8 %all-gather.11.cloned.1.call-start = ((), (), s32[]{:S(2)}) async-start(), calls=%async_computation.10 | async-start | bytes 7077888 | tf_op jit(solution)/shard_map/all_gather | solution.py:98
  9.5 4.8 copy-start.64
  9.5 5.5 %copy-start.52 = (bf16[256,768]{1,0:T(8,128)(2,1)S(1)}, bf16[256,768]{1,0:T(8,128)(2,1)}, u32[]{:S(2)}) copy-start(bf16[256,768]{1,0:T(8,128)(2,1)} %param.37) | copy-start | bytes 1179652
  9.6 123.6 %all-gather.9.cloned.1.call-start = ((), (), s32[]{:S(2)}) async-start(), calls=%async_computation.9 | async-start | bytes 14155776 | tf_op jit(solution)/shard_map/all_gather | solution.py:98
  13.7 20.2 %copy-start.20 = (bf16[2,176,768]{2,1,0:T(8,128)(2,1)S(1)}, bf16[2,176,768]{2,1,0:T(8,128)(2,1)}, u32[]{:S(2)}) copy-start(bf16[2,176,768]{2,1,0:T(8,128)(2,1)} %param.19) | copy-start | bytes 1622020
  15.0 19.0 %copy-start.65 = (s32[2,176]{1,0:T(2,128)S(1)}, s32[2,176]{1,0:T(2,128)}, u32[]{:S(2)}) copy-start(s32[2,176]{1,0:T(2,128)} %param.21) | copy-start | bytes 4228
  15.0 19.2 %copy-start.69 = (s32[2,512]{1,0:T(2,128)S(1)}, s32[2,512]{1,0:T(2,128)}, u32[]{:S(2)}) copy-start(s32[2,512]{1,0:T(2,128)} %param.22) | copy-start | bytes 12292
  15.8 339.6 %reduce-scatter.5.cloned.1.call-start = ((), (), s32[]{:S(2)}) async-start(), calls=%async_computation.4 | async-start | bytes 14155776 | tf_op jit(solution)/shard_map/reduce_scatter | solution.py:117
  149.8 11.9 %copy-start.14 = (bf16[2,176,768]{1,2,0:T(8,128)(2,1)}, bf16[2,176,768]{1,2,0:T(8,128)(2,1)S(1)}, u32[]{:S(2)}) copy-start(bf16[2,176,768]{1,2,0:T(8,128)(2,1)S(1)} %copy.105) | copy-start | bytes 1622020
  181.6 13.9 %copy-start.8 = (f32[2,176,768]{2,1,0:T(8,128)}, f32[2,176,768]{2,1,0:T(8,128)S(1)}, u32[]{:S(2)}) copy-start(f32[2,176,768]{2,1,0:T(8,128)S(1)} %get-tuple-element.63) | copy-start | bytes 3244036
  201.4 7.3 %copy-start.30 = (pred[2,176,512]{2,1,0:T(8,128)(4,1)S(1)}, pred[2,176,512]{2,1,0:T(8,128)(4,1)}, u32[]{:S(2)}) copy-start(pred[2,176,512]{2,1,0:T(8,128)(4,1)} %broadcast_compare_fusion) | copy-start | bytes 540676
  201.4 7.3 %copy-start.31 = (bf16[2,176,768]{1,2,0:T(8,128)(2,1)S(1)}, bf16[2,176,768]{1,2,0:T(8,128)(2,1)}, u32[]{:S(2)}) copy-start(bf16[2,176,768]{1,2,0:T(8,128)(2,1)} %copy.113) | copy-start | bytes 1622020
  201.4 7.3 %copy-start.41 = (bf16[768,2,512]{2,0,1:T(8,128)(2,1)S(1)}, bf16[768,2,512]{2,0,1:T(8,128)(2,1)}, u32[]{:S(2)}) copy-start(bf16[768,2,512]{2,0,1:T(8,128)(2,1)} %convolution_convert_fusion.2) | copy-start | bytes 4718596
  201.4 7.3 %copy-start.56 = (f32[2,12,176]{2,1,0:T(8,128)S(1)}, f32[2,12,176]{2,1,0:T(8,128)}, u32[]{:S(2)}) copy-start(f32[2,12,176]{2,1,0:T(8,128)} %copy-done.55) | copy-start | bytes 50692
  201.4 13.2 %slice-start = ((s8[8650752]{0:T(1024)(128)(4,1)}), s8[4194304]{0:T(1024)(128)(4,1)S(1)}, s32[]{:S(2)}) async-start(s8[8650752]{0:T(1024)(128)(4,1)} %bitcast.192), calls=%async_computation.11 | async-start | bytes 8388608
  201.5 13.2 %slice-start.1 = ((s8[8650752]{0:T(1024)(128)(4,1)}), s8[4194304]{0:T(1024)(128)(4,1)S(1)}, s32[]{:S(2)}) async-start(s8[8650752]{0:T(1024)(128)(4,1)} %bitcast.192), calls=%async_computation.12 | async-start | bytes 8388608
  208.7 6.0 %slice-start.2 = ((s8[8650752]{0:T(1024)(128)(4,1)}), s8[262144]{0:T(1024)(128)(4,1)S(1)}, s32[]{:S(2)}) async-start(s8[8650752]{0:T(1024)(128)(4,1)} %bitcast.192), calls=%async_computation.13 | async-start | bytes 524288
  230.6 7.7 %slice-start.3 = ((s8[4325376]{0:T(1024)(128)(4,1)}), s8[4194304]{0:T(1024)(128)(4,1)S(1)}, s32[]{:S(2)}) async-start(s8[4325376]{0:T(1024)(128)(4,1)} %bitcast.194), calls=%async_computation.14 | async-start | bytes 8388608
  234.1 11.9 %copy-start.48 = (bf16[2,12,64,176]{3,2,1,0:T(8,128)(2,1)}, bf16[2,12,64,176]{3,2,1,0:T(8,128)(2,1)S(1)}, u32[]{:S(2)}) copy-start(bf16[2,12,64,176]{3,2,1,0:T(8,128)(2,1)S(1)} %convolution_convert_fusion.4) | copy-start | bytes 1622020
  240.5 8.5 %copy-start.38 = (bf16[2,12,64,176]{3,2,1,0:T(8,128)(2,1)}, bf16[2,12,64,176]{3,2,1,0:T(8,128)(2,1)S(1)}, u32[]{:S(2)}) copy-start(bf16[2,12,64,176]{3,2,1,0:T(8,128)(2,1)S(1)} %multiply_convert_fusion.5) | copy-start | bytes 1622020
  241.0 8.9 %copy-start.36 = (bf16[2,12,64,176]{3,2,1,0:T(8,128)(2,1)}, bf16[2,12,64,176]{3,2,1,0:T(8,128)(2,1)S(1)}, u32[]{:S(2)}) copy-start(bf16[2,12,64,176]{3,2,1,0:T(8,128)(2,1)S(1)} %multiply_convert_fusion.6) | copy-start | bytes 1622020
  262.9 157.5 %reduce-scatter.9.cloned.1.call-start = ((), (), s32[]{:S(2)}) async-start(), calls=%async_computation.7 | async-start | bytes 7077888 | tf_op jit(solution)/shard_map/reduce_scatter | solution.py:117
  274.0 148.0 %copy-start.72 = (bf16[768]{0:T(1024)(128)(2,1)S(1)}, bf16[768]{0:T(1024)(128)(2,1)}, u32[]{:S(2)}) copy-start(bf16[768]{0:T(1024)(128)(2,1)} %get-tuple-element.19) | copy-start | bytes 4612
  274.0 148.1 %copy-start.66 = (bf16[768]{0:T(1024)(128)(2,1)S(1)}, bf16[768]{0:T(1024)(128)(2,1)}, u32[]{:S(2)}) copy-start(bf16[768]{0:T(1024)(128)(2,1)} %get-tuple-element.17) | copy-start | bytes 4612
  274.0 148.2 %copy-start.37 = (bf16[2,12,64,176]{3,2,1,0:T(8,128)(2,1)S(1)}, bf16[2,12,64,176]{3,2,1,0:T(8,128)(2,1)}, u32[]{:S(2)}) copy-start(bf16[2,12,64,176]{3,2,1,0:T(8,128)(2,1)} %copy-done.36) | copy-start | bytes 1622020
  274.0 184.0 %reduce-scatter.7.cloned.1.call-start = ((), (), s32[]{:S(2)}) async-start(), calls=%async_computation.5 | async-start | bytes 1966080 | tf_op jit(solution)/shard_map/reduce_scatter | solution.py:118
  355.5 145.5 %reduce-scatter.11.cloned.1.call-start = ((), (), s32[]{:S(2)}) async-start(), calls=%async_computation.8 | async-start | bytes 983040 | tf_op jit(solution)/shard_map/reduce_scatter | solution.py:118
  420.5 113.0 %all-gather.7.cloned.1.call-start = ((), (), s32[]{:S(2)}) async-start(), calls=%async_computation.6 | async-start | bytes 1966080 | tf_op jit(solution)/shard_map/all_gather | solution.py:119
  (63 other events, 147.7 us)
Sparse Core Ops, SparseCore 0:
  10.6 48.4 all-gather.10
  61.0 72.1 all-gather.8
  263.0 92.3 reduce-scatter.4
  358.7 61.7 reduce-scatter.8
  422.7 35.2 reduce-scatter.6
  460.3 22.3 reduce-scatter.10
  484.3 49.0 all-gather.6

commit v2 on v1

--- a/solution.py
+++ b/solution.py
@@ -1,9 +1,14 @@
+import functools
+
 import jax
 import jax.numpy as jnp
 from jax import lax
+from jax.experimental import pallas as pl
+from jax.experimental.pallas import tpu as pltpu
 from jax.sharding import PartitionSpec as P
 
 HD = 64
+MODEL = 768
 
 
 EPSILON = 1e-06
@@ -43,30 +48,27 @@
     return tensor.reshape(tensor.shape[0], tensor.shape[1], -1)
 
 
-def masked_scores(queries, keys_all, allowed):
-    raw_scores = jnp.einsum(
+def attention_probs(queries, keys_all, allowed):
+    scores = jnp.einsum(
         "rqhd,rkhd->rhqk",
         split_heads(queries),
         split_heads(keys_all),
         preferred_element_type=jnp.float32,
-    ) * HD ** (-0.5)
-    return jnp.where(allowed[:, None], raw_scores, MASKED)
+    )
+    scores = jnp.where(allowed[:, None], scores, MASKED)
+    return jax.nn.softmax(scores, axis=-1)
 
 
 def attend_forward(queries, keys_all, values, allowed):
-    scores = masked_scores(queries, keys_all, allowed)
-    maxima = jnp.max(scores, axis=-1, keepdims=True)
-    log_total = maxima + jnp.log(jnp.sum(jnp.exp(scores - maxima), axis=-1, keepdims=True))
-    weights_low = jnp.exp(scores - log_total).astype(jnp.bfloat16)
+    probs = attention_probs(queries, keys_all, allowed).astype(jnp.bfloat16)
     mixture = jnp.einsum(
-        "rhqk,rkhd->rqhd", weights_low, split_heads(values), preferred_element_type=jnp.float32
-    )
-    return (merge_heads(mixture).astype(jnp.bfloat16), log_total)
-
-
-def attend_backward(queries, keys_all, values, allowed, log_total, grad_mix):
-    scores = masked_scores(queries, keys_all, allowed)
-    weights_full = jnp.exp(scores - log_total)
+        "rhqk,rkhd->rqhd", probs, split_heads(values), preferred_element_type=jnp.float32
+    )
+    return merge_heads(mixture).astype(jnp.bfloat16)
+
+
+def attend_backward(queries, keys_all, values, allowed, grad_mix):
+    weights_full = attention_probs(queries, keys_all, allowed)
     grad_heads = split_heads(grad_mix)
     grad_values = jnp.einsum(
         "rhqk,rqhd->rkhd",
@@ -85,7 +87,7 @@
     ) * HD ** (-0.5)
     grad_keys = jnp.einsum(
         "rhqk,rqhd->rkhd", grad_scores, split_heads(queries), preferred_element_type=jnp.float32
-    ) * HD ** (-0.5)
+    )
     return (
         merge_heads(grad_queries).astype(jnp.bfloat16),
         merge_heads(grad_keys).astype(jnp.bfloat16),
@@ -126,35 +128,40 @@
     return parts
 
 
-def micro_step(
-    dec_rows, enc_rows, seg_rows_dec, seg_rows_enc, grad_rows, get_self, get_cross, get_ffn
-):
-    position = jnp.arange(seg_rows_dec.shape[1])
-    causal = position[:, None] >= position[None, :]
-    self_ok = (seg_rows_dec[:, :, None] == seg_rows_dec[:, None, :]) & causal[None]
-    cross_ok = seg_rows_dec[:, :, None] == seg_rows_enc[:, None, :]
+def forward(dec_rows, enc_rows, self_ok, cross_ok, get_self, get_cross):
     gain_a, wq_a, wk_a, wv_a, wo_a = get_self()
     dec_float = dec_rows.astype(jnp.float32)
     normed_a = rms_forward(dec_float, gain_a.astype(jnp.float32)).astype(jnp.bfloat16)
-    query_a = project(normed_a, wq_a).astype(jnp.bfloat16)
+    query_a = (project(normed_a, wq_a) * HD ** (-0.5)).astype(jnp.bfloat16)
     keys_a = project(normed_a, wk_a).astype(jnp.bfloat16)
     values_a = project(normed_a, wv_a).astype(jnp.bfloat16)
-    mix_a, total_a = attend_forward(query_a, keys_a, values_a, self_ok)
+    mix_a = attend_forward(query_a, keys_a, values_a, self_ok)
     after_self = dec_float + project(mix_a, wo_a)
     gain_c, wq_c, wk_c, wv_c, wo_c = get_cross()
     normed_c = rms_forward(after_self, gain_c.astype(jnp.float32)).astype(jnp.bfloat16)
-    query_c = project(normed_c, wq_c).astype(jnp.bfloat16)
+    query_c = (project(normed_c, wq_c) * HD ** (-0.5)).astype(jnp.bfloat16)
     keys_c = project(enc_rows, wk_c).astype(jnp.bfloat16)
     values_c = project(enc_rows, wv_c).astype(jnp.bfloat16)
-    mix_c, total_c = attend_forward(query_c, keys_c, values_c, cross_ok)
+    mix_c = attend_forward(query_c, keys_c, values_c, cross_ok)
     after_cross = after_self + project(mix_c, wo_c)
+    return (
+        (normed_a, query_a, keys_a, values_a, mix_a, normed_c, query_c, mix_c),
+        (keys_c, values_c),
+        (after_self, after_cross),
+    )
+
+
+def backward(dec_rows, enc_rows, self_ok, cross_ok, grad_rows, kept, get_self, get_cross, get_ffn):
+    (normed_a, query_a, keys_a, values_a, mix_a, normed_c, query_c, mix_c) = kept[0]
+    keys_c, values_c = kept[1]
+    after_self, after_cross = kept[2]
+    dec_float = dec_rows.astype(jnp.float32)
     gain_f, gate_w, up_w, down_w = get_ffn()
     normed_f = rms_forward(after_cross, gain_f.astype(jnp.float32)).astype(jnp.bfloat16)
     gate_pre = project(normed_f, gate_w)
     up_pre = project(normed_f, up_w)
     hidden_low = (jax.nn.gelu(gate_pre, approximate=True) * up_pre).astype(jnp.bfloat16)
     dec_result = (after_cross + project(hidden_low, down_w)).astype(jnp.bfloat16)
-    gain_f, gate_w, up_w, down_w = get_ffn()
     grad_res = grad_rows.astype(jnp.float32)
     grad_branch = grad_res.astype(jnp.bfloat16)
     grad_down = weight_grad(hidden_low, grad_branch)
@@ -175,7 +182,7 @@
     grad_wo_c = weight_grad(mix_c, grad_branch)
     grad_mix = input_grad(grad_branch, wo_c).astype(jnp.bfloat16)
     grad_query, grad_keys, grad_values = attend_backward(
-        query_c, keys_c, values_c, cross_ok, total_c, grad_mix
+        query_c, keys_c, values_c, cross_ok, grad_mix
     )
     grad_wq_c = weight_grad(normed_c, grad_query)
     grad_wk_c = weight_grad(enc_rows, grad_keys)
@@ -189,7 +196,7 @@
     grad_wo_a = weight_grad(mix_a, grad_branch)
     grad_mix = input_grad(grad_branch, wo_a).astype(jnp.bfloat16)
     grad_query, grad_keys, grad_values = attend_backward(
-        query_a, keys_a, values_a, self_ok, total_a, grad_mix
+        query_a, keys_a, values_a, self_ok, grad_mix
     )
     grad_wq_a = weight_grad(normed_a, grad_query)
     grad_wk_a = weight_grad(normed_a, grad_keys)
@@ -216,6 +223,448 @@
         grad_down,
     )
     return (dec_result, grad_dec_rows, grad_enc_rows, full_grads)
+
+
+def dot_nn(left, right):
+    return lax.dot_general(left, right, (((1,), (0,)), ((), ())), preferred_element_type=jnp.float32)
+
+
+def dot_nt(left, right):
+    return lax.dot_general(left, right, (((1,), (1,)), ((), ())), preferred_element_type=jnp.float32)
+
+
+def dot_tn(left, right):
+    return lax.dot_general(left, right, (((0,), (0,)), ((), ())), preferred_element_type=jnp.float32)
+
+
+def flip(index, step):
+    return index + step - 2 * step * ((index // step) % 2)
+
+
+class Place:
+    def __init__(self):
+        self.dp = lax.axis_index("dp")
+        self.fs = lax.axis_index("fsdp")
+        self.core = self.fs % 2
+        self.x = (self.fs // 2) % 2
+        self.y = (self.fs // 4) % 2
+
+    def to_core(self):
+        return (self.dp, flip(self.fs, 1))
+
+    def to_x(self):
+        return (self.dp, flip(self.fs, 2))
+
+    def to_y(self):
+        return (self.dp, flip(self.fs, 4))
+
+    def to_z(self, step):
+        return (flip(self.dp, step), self.fs)
+
+
+def remote(source, target, send_sem, recv_sem, device):
+    return pltpu.make_async_remote_copy(
+        src_ref=source,
+        dst_ref=target,
+        send_sem=send_sem,
+        recv_sem=recv_sem,
+        device_id=device,
+        device_id_type=pl.DeviceIdType.MESH,
+    )
+
+
+def greet(devices):
+    barrier = pltpu.get_barrier_semaphore()
+    for device in devices:
+        pl.semaphore_signal(
+            barrier, inc=1, device_id=device, device_id_type=pl.DeviceIdType.MESH
+        )
+    pl.semaphore_wait(barrier, len(devices))
+
+
+class Gather:
+    def __init__(self, place, shards, wholes, chunks, sems):
+        self.place = place
+        self.shards = shards
+        self.wholes = wholes
+        self.chunks = chunks
+        self.send_sems, self.recv_sems, self.own_sems = sems
+        even = 1 - place.dp % 2
+        fs = place.fs
+        self.first = even * flip(fs, 2) + (1 - even) * flip(fs, 4)
+        self.second = even * flip(fs, 4) + (1 - even) * flip(fs, 2)
+        self.cross = flip(flip(fs, 2), 4)
+        self.peers = [
+            (place.dp, self.first),
+            (place.dp, self.second),
+            place.to_z(1),
+            place.to_core(),
+        ]
+
+    def block(self, index, owner):
+        which, start, rows = self.chunks[index]
+        count = self.shards[which].shape[0]
+        return self.wholes[which].at[pl.ds(owner * count + start, rows)]
+
+    def copy(self, index, flow, owner, device, own=False):
+        which, start, rows = self.chunks[index]
+        source = self.shards[which].at[pl.ds(start, rows)] if own else self.block(index, owner)
+        return remote(
+            source,
+            self.block(index, owner),
+            self.send_sems.at[index, flow],
+            self.recv_sems.at[index, flow],
+            device,
+        )
+
+    def begin(self, index):
+        fs = self.place.fs
+        self.copy(index, 0, fs, self.peers[0], own=True).start()
+        self.copy(index, 3, fs, self.peers[3], own=True).start()
+
+    def keep(self, index):
+        which, start, rows = self.chunks[index]
+        return pltpu.make_async_copy(
+            self.shards[which].at[pl.ds(start, rows)],
+            self.block(index, self.place.fs),
+            self.own_sems.at[index],
+        )
+
+    def relay_first(self, index):
+        self.copy(index, 0, self.first, self.peers[0]).wait_recv()
+        self.copy(index, 1, self.first, self.peers[1]).start()
+        self.copy(index, 2, self.first, self.peers[2]).start()
+        self.copy(index, 4, self.first, self.peers[3]).start()
+
+    def relay_rest(self, index):
+        self.copy(index, 1, self.cross, self.peers[1]).wait_recv()
+        self.copy(index, 5, self.cross, self.peers[3]).start()
+        self.copy(index, 2, self.second, self.peers[2]).wait_recv()
+        self.copy(index, 6, self.second, self.peers[3]).start()
+
+    def finish(self, index):
+        self.keep(index).wait()
+        for flow, owner in ((3, self.place.fs), (4, self.first), (5, self.cross), (6, self.second)):
+            self.copy(index, flow, flip(owner, 1), self.peers[3]).wait_recv()
+
+    def drain(self):
+        fs = self.place.fs
+        owners = (fs, self.first, self.first, fs, self.first, self.cross, self.second)
+        targets = (0, 1, 2, 3, 3, 3, 3)
+        for index in range(len(self.chunks)):
+            for flow in range(7):
+                self.copy(
+                    index, flow, owners[flow], self.peers[targets[flow]], own=flow in (0, 3)
+                ).wait_send()
+
+
+def row_blocks(body, rows, step):
+    def run(index, carry):
+        body(pl.ds(pl.multiple_of(index * step, step), step))
+        return carry
+
+    lax.fori_loop(0, rows // step, run, 0)
+
+
+def norm_rows(source, gain, target, rows, step=32):
+    def body(block):
+        values = source[block, :].astype(jnp.float32)
+        scale = lax.rsqrt(jnp.mean(values * values, axis=-1, keepdims=True) + EPSILON)
+        target[block, :] = (values * scale * gain).astype(target.dtype)
+
+    row_blocks(body, rows, step)
+
+
+def lane_halves():
+    lane = lax.broadcasted_iota(jnp.int32, (1, 2 * HD), 1)
+    low_half = (lane < HD).astype(jnp.float32)
+    return low_half.astype(jnp.bfloat16), (1.0 - low_half).astype(jnp.bfloat16)
+
+
+def make_masks(seg_dec, seg_enc, mask_self, mask_cross):
+    rows, length = seg_dec.shape
+    query = lax.broadcasted_iota(jnp.int32, (length, length), 0)
+    key = lax.broadcasted_iota(jnp.int32, (length, length), 1)
+    for row in range(rows):
+        along = seg_dec[row : row + 1, :].astype(jnp.float32)
+        down = jnp.sum(jnp.where(query == key, along, 0.0), axis=1, keepdims=True)
+        same = jnp.where((down == along) & (key <= query), 1.0, 0.0)
+        mask_self[row] = same
+        enc = seg_enc[row : row + 1, :].astype(jnp.float32)
+        mask_cross[row] = jnp.where(down == enc, 1.0, 0.0)
+
+
+def softmax_rows(queries, keys, mask):
+    scores = jnp.where(mask > 0.0, dot_nt(queries, keys), MASKED)
+    powers = jnp.exp(scores - jnp.max(scores, axis=-1, keepdims=True))
+    return powers * (1.0 / jnp.sum(powers, axis=-1, keepdims=True))
+
+
+def attend_pairs(queries, keys, values, mask, target, len_q, len_k, first, last):
+    pairs = queries.shape[1] // (2 * HD)
+
+    def body(index, carry):
+        row, pair = index // pairs, index % pairs
+        cols = pl.ds(pl.multiple_of(pair * 2 * HD, 2 * HD), 2 * HD)
+        at_q = pl.ds(pl.multiple_of(row * len_q, 16), len_q)
+        at_k = pl.ds(pl.multiple_of(row * len_k, 16), len_k)
+        both_q, both_k, both_v = queries[at_q, cols], keys[at_k, cols], values[at_k, cols]
+        allowed = mask[row]
+        total = None
+        for half in lane_halves():
+            probs = softmax_rows(both_q * half, both_k, allowed).astype(jnp.bfloat16)
+            part = dot_nn(probs, both_v * half)
+            total = part if total is None else total + part
+        target[at_q, cols] = total.astype(jnp.bfloat16)
+        return carry
+
+    lax.fori_loop(first, last, body, 0)
+
+
+def interleave(work, steps):
+    now = 0.0
+    done = 0
+
+    def do_step():
+        nonlocal now, done
+        ready, action = steps[done]
+        action()
+        now = max(now, ready) + 0.2
+        done += 1
+
+    for needed, duration, action in work:
+        while done <= needed:
+            do_step()
+        while done < len(steps) and steps[done][0] <= now:
+            do_step()
+        action()
+        now += duration
+    while done < len(steps):
+        do_step()
+
+
+FORWARD_ORDER = ("wq_a", "wk_a", "wv_a", "wo_a", "wk_c", "wv_c", "wq_c", "wo_c", "gate", "up", "down")
+LINK_BYTES_PER_US = 45000.0
+WINDOW = 3
+
+
+def gain_row(gains, which, count):
+    width = MODEL // count
+    return jnp.concatenate(
+        [gains[8 * owner + which : 8 * owner + which + 1, 0:width] for owner in range(count)], axis=1
+    )
+
+
+def forward_kernel(dims, *refs):
+    shard_refs = refs[0:12]
+    dec_hbm, enc_hbm, seg_dec, seg_enc = refs[12:16]
+    whole_refs = refs[16:28]
+    small_out, large_out, float_out = refs[28:31]
+    (weights, small, large, floats, dec, enc, gains, mask_self, mask_cross) = refs[31:40]
+    send_sems, recv_sems, own_sems, load_sems, store_sems = refs[40:45]
+    rows, len_q, len_k, count = dims
+    tokens, enc_tokens = rows * len_q, rows * len_k
+
+    place = Place()
+    chunks = [(11, 0, 8)]
+    for which, shard in enumerate(shard_refs[0:11]):
+        height = shard.shape[0]
+        pieces = 1 if which < 8 else (2 if which < 10 else 4)
+        for piece in range(pieces):
+            chunks.append((which, piece * height // pieces, height // pieces))
+    gather = Gather(place, shard_refs, whole_refs, chunks, (send_sems, recv_sems, own_sems))
+
+    loads = {}
+
+    def load(name, source, target, sem):
+        loads[name] = pltpu.make_async_copy(source, target, load_sems.at[sem])
+        loads[name].start()
+
+    load("dec", dec_hbm, dec, 0)
+    load("enc", enc_hbm, enc, 1)
+    greet(gather.peers)
+    for index in range(WINDOW):
+        gather.begin(index)
+    for index in range(len(chunks)):
+        gather.keep(index).start()
+
+    timed = []
+    clock = 3.0
+    for index, (which, start, height) in enumerate(chunks):
+        bytes_sent = height * shard_refs[which].shape[1] * 2
+        clock += bytes_sent / LINK_BYTES_PER_US
+        again = clock + bytes_sent / LINK_BYTES_PER_US + 3.0
+
+        def first_step(index=index):
+            gather.relay_first(index)
+            if index + WINDOW < len(chunks):
+                gather.begin(index + WINDOW)
+
+        def rest_step(index=index):
+            gather.relay_rest(index)
+
+        def last_step(index=index, which=which):
+            gather.finish(index)
+            if which < 8:
+                load(which, whole_refs[which], weights.at[which], 2 + which)
+            if which == 11:
+                load("gains", whole_refs[11], gains, 10)
+
+        timed.append((clock, 0, index, first_step))
+        timed.append((again, 1, index, rest_step))
+        timed.append((again + 2.0, 2, index, last_step))
+    timed.sort(key=lambda item: item[:3])
+    steps = [(item[0], item[3]) for item in timed]
+    where = {item[1:3]: position for position, item in enumerate(timed)}
+    whole_at = {}
+    for index, (which, _, _) in enumerate(chunks):
+        whole_at[which] = where[(2, index)]
+
+    stores = []
+
+    def store(source, target):
+        stores.append(pltpu.make_async_copy(source, target, store_sems.at[len(stores)]))
+        stores[-1].start()
+
+    def keep_small(index):
+        store(small.at[index], small_out.at[index])
+
+    def project(acts, which, target, scale=None):
+        loads[which].wait()
+        result = dot_nn(acts[...], weights[which])
+        if scale is not None:
+            result = result * scale
+        target[...] = result.astype(target.dtype)
+
+    work = []
+
+    def masks():
+        make_masks(seg_dec, seg_enc, mask_self, mask_cross)
+        loads["dec"].wait()
+
+    def norm_self():
+        loads["gains"].wait()
+        norm_rows(dec, gain_row(gains, 0, count), small.at[0], tokens)
+        keep_small(0)
+
+    def query_self():
+        project(small.at[0], 0, small.at[1], HD ** (-0.5))
+        keep_small(1)
+
+    def key_self():
+        project(small.at[0], 1, small.at[2])
+        keep_small(2)
+
+    def value_self():
+        project(small.at[0], 2, small.at[3])
+        keep_small(3)
+
+    def mix_self(first, last):
+        attend_pairs(
+            small.at[1], small.at[2], small.at[3], mask_self, small.at[4], len_q, len_q, first, last
+        )
+
+    def out_self():
+        keep_small(4)
+        loads[3].wait()
+        floats[0] = dec[...].astype(jnp.float32) + dot_nn(small[4], weights[3])
+        store(floats.at[0], float_out.at[0])
+        norm_rows(floats.at[0], gain_row(gains, 1, count), small.at[5], tokens)
+        keep_small(5)
+
+    def key_cross():
+        loads["enc"].wait()
+        project(enc, 4, large.at[0])
+        store(large.at[0], large_out.at[0])
+
+    def value_cross():
+        project(enc, 5, large.at[1])
+        store(large.at[1], large_out.at[1])
+
+    def query_cross():
+        project(small.at[5], 6, small.at[6], HD ** (-0.5))
+        keep_small(6)
+
+    def mix_cross(first, last):
+        attend_pairs(
+            small.at[6], large.at[0], large.at[1], mask_cross, small.at[7], len_q, len_k, first, last
+        )
+
+    def out_cross():
+        keep_small(7)
+        loads[7].wait()
+        floats[1] = floats[0] + dot_nn(small[7], weights[7])
+        store(floats.at[1], float_out.at[1])
+        norm_rows(floats.at[1], gain_row(gains, 2, count), small.at[8], tokens)
+        keep_small(8)
+
+    total = rows * (MODEL // (2 * HD))
+    work.append((-1, 1.0, masks))
+    work.append((whole_at[11], 1.0, norm_self))
+    work.append((whole_at[0], 1.2, query_self))
+    work.append((whole_at[1], 1.2, key_self))
+    work.append((whole_at[2], 1.2, value_self))
+    for part in range(2):
+        bounds = (part * total // 2, (part + 1) * total // 2)
+        work.append((-1, 2.0, functools.partial(mix_self, *bounds)))
+    work.append((whole_at[3], 2.0, out_self))
+    work.append((whole_at[4], 2.5, key_cross))
+    work.append((whole_at[5], 2.5, value_cross))
+    work.append((whole_at[6], 1.2, query_cross))
+    for part in range(4):
+        bounds = (part * total // 4, (part + 1) * total // 4)
+        work.append((-1, 2.5, functools.partial(mix_cross, *bounds)))
+    work.append((whole_at[7], 2.0, out_cross))
+    interleave(work, steps)
+    gather.drain()
+    for copy in stores:
+        copy.wait()
+
+
+def forward_call(shards, gain_tile, dec, enc, seg_dec, seg_enc):
+    rows, len_q = seg_dec.shape
+    len_k = seg_enc.shape[1]
+    count = lax.axis_size("fsdp")
+    tokens, enc_tokens = rows * len_q, rows * len_k
+    wholes = [
+        jax.ShapeDtypeStruct((shard.shape[0] * count, shard.shape[1]), shard.dtype)
+        for shard in (*shards, gain_tile)
+    ]
+    n_chunks = 17
+    half = jnp.bfloat16
+    in_any = pl.BlockSpec(memory_space=pl.ANY)
+    in_vmem = pl.BlockSpec(memory_space=pltpu.VMEM)
+    return pl.pallas_call(
+        functools.partial(forward_kernel, (rows, len_q, len_k, count)),
+        out_shape=wholes
+        + [
+            jax.ShapeDtypeStruct((9, tokens, MODEL), half),
+            jax.ShapeDtypeStruct((2, enc_tokens, MODEL), half),
+            jax.ShapeDtypeStruct((2, tokens, MODEL), jnp.float32),
+        ],
+        in_specs=[in_any] * 14 + [in_vmem] * 2,
+        out_specs=[in_any] * 15,
+        scratch_shapes=[
+            pltpu.VMEM((8, MODEL, MODEL), half),
+            pltpu.VMEM((9, tokens, MODEL), half),
+            pltpu.VMEM((2, enc_tokens, MODEL), half),
+            pltpu.VMEM((2, tokens, MODEL), jnp.float32),
+            pltpu.VMEM((tokens, MODEL), half),
+            pltpu.VMEM((enc_tokens, MODEL), half),
+            pltpu.VMEM((8 * count, 128), jnp.float32),
+            pltpu.VMEM((rows, len_q, len_q), jnp.float32),
+            pltpu.VMEM((rows, len_q, len_k), jnp.float32),
+            pltpu.SemaphoreType.DMA((n_chunks, 7)),
+            pltpu.SemaphoreType.DMA((n_chunks, 7)),
+            pltpu.SemaphoreType.DMA((n_chunks,)),
+            pltpu.SemaphoreType.DMA((11,)),
+            pltpu.SemaphoreType.DMA((13,)),
+        ],
+        compiler_params=pltpu.CompilerParams(
+            collective_id=0, has_side_effects=True, vmem_limit_bytes=60 * 1024 * 1024
+        ),
+        name="gather_forward",
+    )(*shards, gain_tile, dec, enc, seg_dec, seg_enc)
 
 
 def body(
@@ -240,14 +689,45 @@
     w_down,
 ):
     narrow = (wq_self, wk_self, wv_self, wo_self, wq_cross, wk_cross, wv_cross, wo_cross, w_down)
-    gain_a, gain_c, gain_f = gather_group((gain_self, gain_cross, gain_ffn))
-    full = gather_group(narrow)
-    gate_full, up_full = gather_group((w_gate, w_up))
-    get_self = lambda: (gain_a, *full[0:4])
-    get_cross = lambda: (gain_c, *full[4:8])
-    get_ffn = lambda: (gain_f, gate_full, up_full, full[8])
-    result_rows, grad_rows_dec, grad_rows_enc, grads = micro_step(
-        dec_in, enc_out, seg_dec, seg_enc, out_grad, get_self, get_cross, get_ffn
+    position = jnp.arange(seg_dec.shape[1])
+    causal = position[:, None] >= position[None, :]
+    self_ok = (seg_dec[:, :, None] == seg_dec[:, None, :]) & causal[None]
+    cross_ok = seg_dec[:, :, None] == seg_enc[:, None, :]
+    if lax.axis_size("fsdp") == 8 and lax.axis_size("dp") % 2 == 0:
+        gain_tile = jnp.pad(
+            jnp.stack([gain_self, gain_cross, gain_ffn]).astype(jnp.float32),
+            ((0, 5), (0, 128 - gain_self.shape[0])),
+        )
+        got = forward_call(
+            (wq_self, wk_self, wv_self, wo_self)
+            + (wk_cross, wv_cross, wq_cross, wo_cross, w_gate, w_up, w_down),
+            gain_tile,
+            dec_in.reshape(-1, MODEL),
+            enc_out.reshape(-1, MODEL),
+            seg_dec,
+            seg_enc,
+        )
+        gains = got[11].reshape(-1, 8, 128)[:, :3, : gain_self.shape[0]].astype(jnp.bfloat16)
+        gain_a, gain_c, gain_f = (gains[:, g].reshape(-1) for g in range(3))
+        get_self = lambda: (gain_a, *got[0:4])
+        get_cross = lambda: (gain_c, got[6], got[4], got[5], got[7])
+        get_ffn = lambda: (gain_f, got[8], got[9], got[10])
+        small = [got[12][index].reshape(dec_in.shape) for index in range(8)]
+        kept = (
+            small,
+            tuple(got[13][index].reshape(enc_out.shape) for index in range(2)),
+            tuple(got[14][index].reshape(dec_in.shape) for index in range(2)),
+        )
+    else:
+        gain_a, gain_c, gain_f = gather_group((gain_self, gain_cross, gain_ffn))
+        full = gather_group(narrow)
+        gate_full, up_full = gather_group((w_gate, w_up))
+        get_self = lambda: (gain_a, *full[0:4])
+        get_cross = lambda: (gain_c, *full[4:8])
+        get_ffn = lambda: (gain_f, gate_full, up_full, full[8])
+        kept = forward(dec_in, enc_out, self_ok, cross_ok, get_self, get_cross)
+    result_rows, grad_rows_dec, grad_rows_enc, grads = backward(
+        dec_in, enc_out, self_ok, cross_ok, out_grad, kept, get_self, get_cross, get_ffn
     )
     gains = reduce_group((grads[0], grads[5], grads[10]), (gain_self, gain_cross, gain_ffn))
     wide = reduce_group(grads[11:13], (w_gate, w_up))

time: 549 us -> 500 us (0.911); the launches traced: 545 us -> 490 us
  waiting for transfers between devices: 267 us -> 177 us
  Pallas kernels: 0 us -> 79.2 us
  matrix products: 98.7 us -> 67.1 us
  blocking collectives: 77.3 us -> 61.6 us
    all_gather x2 -> x0, waiting for transfers between devices: 91.4 us -> none  [gather_group(): whole = lax.all_gather(joined, 'fsdp', axis=0, tiled=False)]
    pallas_call x0 -> x1, Pallas kernels: none -> 79.2 us  [forward_call(): pl.pallas_call(functools.partial(forward_kernel, (rows, len_q, len_k, cou...]
    another operation x0 -> x9, local copies, waits for them, and re-layouts: none -> 18.7 us  [split_heads(): return tensor.reshape(tensor.shape[0], tensor.shape[1], -1, HD)]
    unnamed x4 -> x3, blocking collectives: 48.6 us -> 32.7 us
    dot_general x11 -> x3, matrix products: 20.7 us -> 7.96 us  [project(): jnp.einsum('rld,dn->rln', acts, weight, preferred_element_type=jnp.float32)]
    dot_general x2, matrix products: 10.7 us -> 2.46 us  [attend_backward(): jnp.einsum('rhqk,rqhd->rkhd', weights_full.astype(jnp.bfloat16), grad_hea...]
    dot_general x4 -> x1, matrix products: 8.2 us -> 1.33 us  [attention_probs(): jnp.einsum('rqhd,rkhd->rhqk', split_heads(queries), split_heads(keys_all)...]
    convert_element_type x9 -> x5, local copies, waits for them, and re-layouts: 9.72 us -> 3.64 us  [the longest x1 2.27 us: backward(): grad_mix = input_grad(grad_branch, wo_a).astype(jnp.bfloat16)]
  transfers between devices with their start and end apart: 7 -> 5, of which waited for: 6 -> 3; matrix products, arithmetic and copies ran while one was open for 8% -> 6% of each run, Pallas kernels for 0% -> 0%
where the time goes in v2:
time: 500 us; the launch traced here: 490 us
  waiting for transfers between devices  177 us (35%)
  Pallas kernels  79.2 us (16%)
  matrix products  67.1 us (13%)
  blocking collectives  61.6 us (12%)
  local copies, waits for them, and re-layouts  58.7 us (12%)
  other arithmetic  30.2 us (6%)
  between operations  16.1 us (3%)
    reduce_scatter x2, waiting for transfers between devices, reduce_group(): owned = lax.psum_scatter(joined, 'fsdp', scatter_dimension=0, tiled=False)  147 us
    pallas_call x1, Pallas kernels, forward_call(): pl.pallas_call(functools.partial(forward_kernel, (rows, len_q, len_k, cou...  79.2 us
    unnamed x3, blocking collectives  32.7 us
    reduce_scatter x2, waiting for transfers between devices, reduce_group(): quarter = lax.psum_scatter(owned, 'dp', scatter_dimension=0, tiled=True)  30.5 us
    all_gather x1, blocking collectives, reduce_group(): summed = lax.all_gather(quarter, 'dp', axis=0, tiled=True)  28.9 us
    dot_general x11, matrix products, input_grad(): jnp.einsum('rln,dn->rld', grad_out, weight, preferred_element_type=jnp.fl...  23 us
    unnamed x137, local copies, waits for them, and re-layouts  21.4 us
    another operation x9, local copies, waits for them, and re-layouts, split_heads(): return tensor.reshape(tensor.shape[0], tensor.shape[1], -1, HD)  18.7 us
  transfers between devices with their start and end apart: 5, of which 3 were waited for; matrix products, arithmetic and copies ran while one was open for 6% of the time, Pallas kernels for 0%

profile of v2, /device:TPU:0, one launch (start us, length us, event | category | flops | bytes accessed | tf_op | source)
XLA Modules:
  0.0 490.4 jit_solution(16630135298828452324)
XLA Ops:
  10.1 79.2 %gather_forward.1 = (bf16[768,768]{1,0:T(8,128)(2,1)}, bf16[768,768]{1,0:T(8,128)(2,1)}, bf16[768,768]{1,0:T(8,128)(2,1)}, bf16[768,768]{1,0:T(8,128)(2,1)}, bf1...) custom-call(bf16[96,768]{1,0:T(8,128)(2,1)} %refs_0_.1, ...), custom_call_target="tpu_custom_call" | custom-call | tf_op jit(solution)/shard_map/gather_forward/pallas_call | solution.py:637
  89.3 2.8 multiply_reduce_fusion.5
  92.3 3.4 fusion.24
  98.0 4.6 fusion.33
  104.1 2.5 multiply_reduce_fusion.2
  106.8 4.1 fusion.100
  112.8 3.5 fusion.101
  118.0 2.9 reshape_reshape_squeeze.22
  120.9 2.3 fusion.69
  125.9 2.6 copy.107
  128.6 3.8 reshape_reshape_squeeze.24
  133.7 4.8 fusion.103
  138.5 5.0 %multiply_reduce_fusion = (f32[2,12,176]{2,1,0:T(8,128)S(1)}, f32[2,12,176,512]{3,2,1,0:T(8,128)S(1)}) fusion(f32[2,12,176,512]{3,2,1,0:T(8,128)S(1)} %get-tuple-element.90, f32[2,12,176]{2,1,0:T(8,128)S(1)} %get-tuple-element.89, bf16[2,176,12,64]{1,3,2,0:T(8,128)(2,1)} %bitcast.221, bf16[2,512,12,64]{1,0,3,2:T(2,128)(2,1)} %reshape_reshape_squeeze.24), kind=kOutput, calls=%fused_computation.3 | convolution fusion | flops 283307904 | bytes 19448832 | tf_op jit(solution)/shard_map/rqhd,rkhd->rhqk/dot_general | solution.py:79
  154.9 2.8 copy.113
  160.8 2.3 copy.115
  163.1 2.7 reshape.268
  165.8 4.7 fusion.104
  170.6 3.9 multiply_reduce_fusion.1
  208.5 3.3 bitcast_convert_fusion
  213.7 4.8 pad_maximum_fusion
  218.6 81.7 %reduce-scatter.5.cloned.1.call-done = bf16[1,1024,768]{2,1,0:T(8,128)(2,1)} async-done(((bf16[8,1024,768]{2,1,0:T(8,128)(2,1)}), bf16[1,1024,768]{2,1,0:T(8,128)(2,1)}) %reduce-scatter.5.cloned.1.call-update) | async-done | bytes 1572880 | tf_op jit(solution)/shard_map/reduce_scatter | solution.py:119
  300.6 64.9 %reduce-scatter.9.cloned.1.call-done = bf16[1,192,2048]{2,1,0:T(8,128)(2,1)} async-done(((bf16[8,192,2048]{2,1,0:T(8,128)(2,1)}), bf16[1,192,2048]{2,1,0:T(8,128)(2,1)}) %reduce-scatter.9.cloned.1.call-update) | async-done | bytes 786448 | tf_op jit(solution)/shard_map/reduce_scatter | solution.py:119
  365.8 2.2 fusion.63
  368.0 2.1 convolution_add_fusion.2
  372.7 30.5 %reduce-scatter.7.cloned.1.call-done = bf16[256,768]{1,0:T(8,128)(2,1)} async-done(((bf16[1024,768]{1,0:T(8,128)(2,1)}), bf16[256,768]{1,0:T(8,128)(2,1)}) %reduce-scatter.7.cloned.1.call-update) | async-done | bytes 393232 | tf_op jit(solution)/shard_map/reduce_scatter | solution.py:120
  405.1 13.7 %all-reduce.2 = bf16[8,288]{1,0:T(8,128)(2,1)S(1)} all-reduce(bf16[8,288]{1,0:T(8,128)(2,1)S(1)} %pad_maximum_fusion.1), channel_id=2, replica_groups=mesh['dp'=4,'fsdp'=8] {'fsdp'}, use_global_device_ids=true, to_apply=%region_15.16.clone | all-reduce | flops 2304 | bytes 9216
  419.5 10.5 %all-reduce.3 = bf16[288]{0:T(512)(128)(2,1)S(1)} all-reduce(bf16[288]{0:T(512)(128)(2,1)S(1)} %dynamic-slice_reduce_fusion), channel_id=3, replica_groups=mesh['dp'=4,'fsdp'=8] {'dp'}, use_global_device_ids=true, to_apply=%region_16.17.clone | all-reduce | flops 288 | bytes 1152
  431.0 8.5 %all-reduce.1 = bf16[288]{0:T(512)(128)(2,1)S(1)} all-reduce(bf16[288]{0:T(512)(128)(2,1)S(1)} %dynamic-update-slice), channel_id=1, replica_groups=mesh['dp'=4,'fsdp'=8] {'dp'}, use_global_device_ids=true, to_apply=%add.1 | all-reduce | flops 288 | bytes 1152
  440.1 3.3 fusion.59
  445.7 3.1 convolution_add_fusion
  448.8 28.9 %all_gather.11 = bf16[192,2048]{1,0:T(8,128)(2,1)S(1)} all-gather(bf16[48,2048]{1,0:T(8,128)(2,1)} %reduce-scatter.11.cloned.1.call-done), channel_id=1, replica_groups=mesh['dp'=4,'fsdp'=8] {'dp'}, dimensions={0}, use_global_device_ids=true | all-gather | bytes 983040 | tf_op jit(solution)/shard_map/all_gather | solution.py:121
  479.0 2.8 slice_convert_fusion.3
  (216 shorter events, 76.2 us)
Async XLA Ops:
  7.2 293.1 %reduce-scatter.5.cloned.1.call-start = ((), (), s32[]{:S(2)}) async-start(), calls=%async_computation.4 | async-start | bytes 14155776 | tf_op jit(solution)/shard_map/reduce_scatter | solution.py:119
  92.1 28.8 %copy-start.5 = (f32[1,352,768]{2,1,0:T(8,128)}, f32[1,352,768]{2,1,0:T(8,128)S(1)}, u32[]{:S(2)}) copy-start(f32[1,352,768]{2,1,0:T(8,128)S(1)} %get-tuple-element.72) | copy-start | bytes 3244036
  92.3 3.6 copy-start.16
  112.8 19.6 %copy-start.10 = (bf16[2,176,12,64]{1,3,2,0:T(8,128)(2,1)}, bf16[2,176,12,64]{1,3,2,0:T(8,128)(2,1)S(1)}, u32[]{:S(2)}) copy-start(bf16[2,176,12,64]{1,3,2,0:T(8,128)(2,1)S(1)} %copy.104) | copy-start | bytes 1622020
  120.8 11.6 %copy-start.2 = (bf16[2,512,12,64]{1,0,3,2:T(2,128)(2,1)}, bf16[2,512,12,64]{1,0,3,2:T(2,128)(2,1)S(1)}, u32[]{:S(2)}) copy-start(bf16[2,512,12,64]{1,0,3,2:T(2,128)(2,1)S(1)} %reshape_reshape_squeeze.22) | copy-start | bytes 4718596
  120.9 3.3 copy-start.33
  138.5 5.0 %copy-start.1 = (f32[2,12,176,512]{3,2,1,0:T(8,128)}, f32[2,12,176,512]{3,2,1,0:T(8,128)S(1)}, u32[]{:S(2)}) copy-start(f32[2,12,176,512]{3,2,1,0:T(8,128)S(1)} %get-tuple-element.90) | copy-start | bytes 25952260
  160.8 5.0 %copy-start.14 = (bf16[2,176,12,64]{1,3,2,0:T(8,128)(2,1)S(1)}, bf16[2,176,12,64]{1,3,2,0:T(8,128)(2,1)}, u32[]{:S(2)}) copy-start(bf16[2,176,12,64]{1,3,2,0:T(8,128)(2,1)} %copy.118) | copy-start | bytes 1622020
  170.6 4.1 slice-start.5
  170.6 4.1 slice-start.6
  176.9 7.8 %copy-start.17 = (bf16[2,12,64,176]{3,2,1,0:T(8,128)(2,1)}, bf16[2,12,64,176]{3,2,1,0:T(8,128)(2,1)S(1)}, u32[]{:S(2)}) copy-start(bf16[2,12,64,176]{3,2,1,0:T(8,128)(2,1)S(1)} %multiply_convert_fusion.4) | copy-start | bytes 1622020
  176.9 5.1 %slice-start.2 = ((s8[8650752]{0:T(1024)(128)(4,1)}), s8[4194304]{0:T(1024)(128)(4,1)S(1)}, s32[]{:S(2)}) async-start(s8[8650752]{0:T(1024)(128)(4,1)} %bitcast.186), calls=%async_computation.11 | async-start | bytes 8388608
  177.7 8.9 %copy-start.19 = (bf16[2,12,64,176]{3,2,1,0:T(8,128)(2,1)}, bf16[2,12,64,176]{3,2,1,0:T(8,128)(2,1)S(1)}, u32[]{:S(2)}) copy-start(bf16[2,12,64,176]{3,2,1,0:T(8,128)(2,1)S(1)} %convolution_convert_fusion.1) | copy-start | bytes 1622020
  177.7 3.4 slice-start.1
  177.7 3.4 copy-start.11
  177.7 4.9 %slice-start.3 = ((s8[8650752]{0:T(1024)(128)(4,1)}), s8[4194304]{0:T(1024)(128)(4,1)S(1)}, s32[]{:S(2)}) async-start(s8[8650752]{0:T(1024)(128)(4,1)} %bitcast.186), calls=%async_computation.12 | async-start | bytes 8388608
  177.7 4.9 %slice-start.4 = ((s8[8650752]{0:T(1024)(128)(4,1)}), s8[262144]{0:T(1024)(128)(4,1)S(1)}, s32[]{:S(2)}) async-start(s8[8650752]{0:T(1024)(128)(4,1)} %bitcast.186), calls=%async_computation.13 | async-start | bytes 524288
  181.1 6.4 %copy-start.36 = (bf16[2,12,64,176]{3,2,1,0:T(8,128)(2,1)}, bf16[2,12,64,176]{3,2,1,0:T(8,128)(2,1)S(1)}, u32[]{:S(2)}) copy-start(bf16[2,12,64,176]{3,2,1,0:T(8,128)(2,1)S(1)} %fusion.43) | copy-start | bytes 1622020
  183.0 7.7 %copy-start.25 = (bf16[2,12,64,512]{3,2,1,0:T(8,128)(2,1)}, bf16[2,12,64,512]{3,2,1,0:T(8,128)(2,1)S(1)}, u32[]{:S(2)}) copy-start(bf16[2,12,64,512]{3,2,1,0:T(8,128)(2,1)S(1)} %convolution_convert_fusion) | copy-start | bytes 4718596
  184.6 8.1 %copy-start.26 = (bf16[2,12,64,512]{3,2,1,0:T(8,128)(2,1)}, bf16[2,12,64,512]{3,2,1,0:T(8,128)(2,1)S(1)}, u32[]{:S(2)}) copy-start(bf16[2,12,64,512]{3,2,1,0:T(8,128)(2,1)S(1)} %fusion.38) | copy-start | bytes 4718596
  207.5 158.0 %reduce-scatter.9.cloned.1.call-start = ((), (), s32[]{:S(2)}) async-start(), calls=%async_computation.7 | async-start | bytes 7077888 | tf_op jit(solution)/shard_map/reduce_scatter | solution.py:119
  208.5 3.3 copy-start.51
  218.5 81.8 %copy-start.9 = (bf16[2,176,768]{2,1,0:T(8,128)(2,1)S(1)}, bf16[2,176,768]{2,1,0:T(8,128)(2,1)}, u32[]{:S(2)}) copy-start(bf16[2,176,768]{2,1,0:T(8,128)(2,1)} %param.19) | copy-start | bytes 1622020
  218.5 147.3 %copy-start.18 = (bf16[2,12,64,176]{3,2,1,0:T(8,128)(2,1)S(1)}, bf16[2,12,64,176]{3,2,1,0:T(8,128)(2,1)}, u32[]{:S(2)}) copy-start(bf16[2,12,64,176]{3,2,1,0:T(8,128)(2,1)} %copy-done.17) | copy-start | bytes 1622020
  218.5 184.6 %reduce-scatter.7.cloned.1.call-start = ((), (), s32[]{:S(2)}) async-start(), calls=%async_computation.5 | async-start | bytes 1966080 | tf_op jit(solution)/shard_map/reduce_scatter | solution.py:120
  300.3 148.5 %reduce-scatter.11.cloned.1.call-start = ((), (), s32[]{:S(2)}) async-start(), calls=%async_computation.8 | async-start | bytes 983040 | tf_op jit(solution)/shard_map/reduce_scatter | solution.py:120
  365.5 113.5 %all-gather.2.cloned.1.call-start = ((), (), s32[]{:S(2)}) async-start(), calls=%async_computation.6 | async-start | bytes 1966080 | tf_op jit(solution)/shard_map/all_gather | solution.py:121
  371.4 31.9 %copy-start.49 = (u32[32]{0:T(128)S(1)}, u32[32]{0:T(128)}, u32[]{:S(2)}) copy-start(u32[32]{0:T(128)} %constant.52) | copy-start | bytes 388
  371.4 32.5 %copy-start.46 = (u32[32]{0:T(128)S(1)}, u32[32]{0:T(128)}, u32[]{:S(2)}) copy-start(u32[32]{0:T(128)} %constant.46) | copy-start | bytes 388
  440.1 3.3 copy-start.6
  440.1 3.3 copy-start.47
  440.1 3.5 copy-start.53
  (35 other events, 65.8 us)
Sparse Core Ops, SparseCore 0:
  207.6 92.6 reduce-scatter.4
  303.7 61.7 reduce-scatter.8
  367.9 35.2 reduce-scatter.6
  405.4 22.3 reduce-scatter.10
  429.3 49.0 all-gather.1
